TPU v7x, 256 devices: a whole 4x4x8 slice. The times are simulated.
256 devices in a mesh: grp: 2 (over core), dev: 128 (over z, x, y).
Axes of the slice: x: 4, y: 4, z: 8, core: 2. Of those that a mesh axis runs over, the one named last changes fastest.
Arguments:
- disp: float32 [3, 512], P(None, 'dev'), may hold values from -6 to 6
- probe: float32 [3, 512], P(None, 'dev'), may hold values from -6 to 6
- strain_disp: float32 [6, 24, 256], P(None, None, 'dev'), may hold values from -1.25 to 1.25
- conn: int32 [8, 256], P(None, 'dev'), may hold values from 0 to 5
- halo_rows: int32 [256], P('dev'), may hold values from 0 to 3
- owner: int32 [256, 1], replicated, may hold values from 0 to 127; in each aligned block of 256 rows (0 to 255, 256 to 511, ...) at most 3 rows name the same one
- counts: int32 [256], replicated, may hold values from 1 to 2
- phase: int32 [128, 32768], P('dev'), may hold values 0 or 1
Outputs:
- point_stress: float32 [6, 256], P(None, 'dev')
- internal_force: float32 [3, 512], P(None, 'dev')
- stiffness_image: float32 [3, 512], P(None, 'dev')
Inputs may be any that keep to these rules, and one draw needn't show every extreme that they name: Each owner has at most 3 points, and some owner has exactly 3. `conn`: local node numbers: the partition's 4 nodes, then 1 nodes received from the partition below, then 1 from the partition above.
All inputs are finite; a program needn't handle non-finite values. No bound on the sum of `phase` on one device may be relied on, other than what follows from the above.
Results may differ from a plain program's by a relative error of at most 0.0003.
Values sent between devices are 32-bit elements; how exact they have to be, the bound alone decides.
A program may use at most 64 MiB of HBM per device.

v0:
```python
import math

import jax
import jax.numpy as jnp
import numpy as np
from jax import lax
from jax.sharding import Mesh
from jax.sharding import PartitionSpec as P

NV = 32
DEV = ("dev_0", "dev_1", "dev_2")


PRECISE = lax.Precision.HIGHEST
ROOT_TWO = 1.4142135623730951
KAPPA_FERRITE = 2.0
SHEAR_FERRITE = 1.0
SOFT_FERRITE = 0.4
KAPPA_MARTENSITE = 2.4
SHEAR_MARTENSITE = 1.3
SOFT_MARTENSITE = 2.5
KAPPA_MEDIUM = 2.2
SHEAR_MEDIUM = 0.75
LAME_MEDIUM = KAPPA_MEDIUM - 2.0 * SHEAR_MEDIUM / 3.0
COUPLING = (LAME_MEDIUM + SHEAR_MEDIUM) / (LAME_MEDIUM + 2.0 * SHEAR_MEDIUM)
UPPER_PAIRS = [(i, j) for i in range(6) for j in range(i, 6)]


def padded(array, sides, width):
    for axis, dim in sides:
        peers, length = (lax.axis_size(axis), array.shape[dim])
        up = [(i, (i + 1) % peers) for i in range(peers - 1)]
        down = [(j, i) for i, j in up]
        last = lax.slice_in_dim(array, length - width, length, axis=dim)
        leading = lax.slice_in_dim(array, 0, width, axis=dim)
        before = lax.ppermute(last, axis, up)
        after = lax.ppermute(leading, axis, down)
        array = jnp.concatenate([before, array, after], axis=dim)
    return array


def whole_of(array, axes, dim):
    if not axes:
        return array
    nearer = lax.all_gather(array, axes[-1], axis=dim, tiled=True)
    return whole_of(nearer, axes[:-1], dim)


def total_of_pieces(array, axis):
    pieces = lax.all_gather(array, axis)
    return pieces.sum(axis=0)


def tangent_table():
    table = np.zeros((6, 6), np.int32)
    for place, pair in enumerate(UPPER_PAIRS):
        table[pair[0], pair[1]] = 6 + place
        table[pair[1], pair[0]] = 6 + place
    return table


def directions(edge):
    index = jnp.arange(edge**3, dtype=jnp.int32)
    parts = [index // (edge * edge), index // edge % edge, index % edge]
    freqs = [jnp.where(k < edge // 2, k, k - edge).astype(jnp.float32) for k in parts]
    length = jnp.sqrt(jnp.maximum(freqs[0] ** 2 + freqs[1] ** 2 + freqs[2] ** 2, 1.0))
    return jnp.stack([f / length for f in freqs])


def dft_tables(edge):
    index = jnp.arange(edge, dtype=jnp.int32)
    turns = index[:, None] * index[None, :] % edge
    angle = 2.0 * math.pi / edge * turns.astype(jnp.float32)
    return (jnp.cos(angle), jnp.sin(angle))


def polarize(tau, normal):
    first, second, third = (normal[0], normal[1], normal[2])
    trac_a = tau[0] * first + tau[5] / ROOT_TWO * second + tau[4] / ROOT_TWO * third
    trac_b = tau[5] / ROOT_TWO * first + tau[1] * second + tau[3] / ROOT_TWO * third
    trac_c = tau[4] / ROOT_TWO * first + tau[3] / ROOT_TWO * second + tau[2] * third
    along = first * trac_a + second * trac_b + third * trac_c
    vec_a = (trac_a - COUPLING * along * first) / SHEAR_MEDIUM
    vec_b = (trac_b - COUPLING * along * second) / SHEAR_MEDIUM
    vec_c = (trac_c - COUPLING * along * third) / SHEAR_MEDIUM
    return jnp.stack(
        [
            first * vec_a,
            second * vec_b,
            third * vec_c,
            (second * vec_c + third * vec_b) / ROOT_TWO,
            (first * vec_c + third * vec_a) / ROOT_TWO,
            (first * vec_b + second * vec_a) / ROOT_TWO,
        ]
    )


def material(strain, kappa, shear, soft):
    unit = jnp.array([1.0, 1.0, 1.0, 0.0, 0.0, 0.0], jnp.float32)[:, None]
    trace = strain[0] + strain[1] + strain[2]
    deviator = strain - unit * (trace / 3.0)
    squares = jnp.sum(deviator * deviator, axis=0)
    factor = 1.0 / jnp.sqrt(1.0 + squares / (soft * soft))
    stress = unit * (kappa * trace) + 2.0 * shear * factor * deviator
    return (stress, deviator, factor)


def rotate(matrix):
    edge = matrix.shape[0]
    return matrix.reshape(edge, 6, edge, edge).transpose(2, 1, 3, 0).reshape(edge, -1)


def axis_pass(real, imag, cos_t, sin_t, sign):
    cos_real = jnp.dot(cos_t, real, precision=PRECISE)
    sin_real = jnp.dot(sin_t, real, precision=PRECISE)
    if imag is None:
        return (rotate(cos_real), rotate(sign * sin_real))
    cos_imag = jnp.dot(cos_t, imag, precision=PRECISE)
    sin_imag = jnp.dot(sin_t, imag, precision=PRECISE)
    return (rotate(cos_real - sign * sin_imag), rotate(cos_imag + sign * sin_real))


def to_spatial(matrix):
    edge = matrix.shape[0]
    return matrix.reshape(edge, 6, edge, edge).transpose(1, 0, 2, 3).reshape(6, -1)


def to_lines(field):
    edge = round_edge(field.shape[1])
    return field.reshape(6, edge, edge * edge).transpose(1, 0, 2).reshape(edge, -1)


def round_edge(voxels):
    edge = 1
    while edge * edge * edge < voxels:
        edge = edge + 1
    return edge


def spectral_step(field, params, tables, normal):
    kappa, shear, soft = params
    cos_t, sin_t = tables
    stress = material(field, kappa, shear, soft)[0]
    real = to_lines(stress)
    imag = None
    for turn in range(3):
        real, imag = axis_pass(real, imag, cos_t, sin_t, -1.0)
    real = to_lines(polarize(to_spatial(real), normal))
    imag = to_lines(polarize(to_spatial(imag), normal))
    real, imag = axis_pass(real, imag, cos_t, sin_t, 1.0)
    real, imag = axis_pass(real, imag, cos_t, sin_t, 1.0)
    last = jnp.dot(cos_t, real, precision=PRECISE) - jnp.dot(sin_t, imag, precision=PRECISE)
    spatial = to_spatial(rotate(last))
    return field - spatial / field.shape[1]


def summarize(field, params):
    kappa, shear, soft = params
    stress, deviator, factor = material(field, kappa, shear, soft)
    unit = jnp.array([1.0, 1.0, 1.0, 0.0, 0.0, 0.0], jnp.float32)
    outer = unit[:, None] * unit[None, :]
    project = jnp.eye(6, dtype=jnp.float32) - outer / 3.0
    weight = 2.0 * shear * factor**3 / (soft * soft)
    tangent = jnp.mean(kappa) * outer + 2.0 * jnp.mean(shear * factor) * project
    tangent = tangent - jnp.dot(deviator * weight, deviator.T, precision=PRECISE) / field.shape[1]
    packed = jnp.stack([tangent[pair[0], pair[1]] for pair in UPPER_PAIRS])
    return jnp.concatenate([jnp.mean(stress, axis=1), packed])


def on_device(disp, probe, strain_disp, conn, halo_rows, owner, counts, phase):
    node_dev = disp.shape[1]
    span = halo_rows.shape[0] // 2
    pt_dev = conn.shape[1]
    total_points = owner.shape[0]
    ext_nodes = node_dev + 2 * span
    slots = (pt_dev + pt_dev // 2 + 7) // 8 * 8
    fields = jnp.concatenate([disp, probe], axis=0)
    row_hits = (halo_rows[:, None] == jnp.arange(node_dev, dtype=jnp.int32)[None, :]).astype(
        jnp.float32
    )
    send_rows = jnp.dot(fields, row_hits.T, precision=PRECISE)
    arrived = padded(send_rows, ((DEV, 1),), span)
    extended = jnp.concatenate([fields, arrived[:, :span], arrived[:, 3 * span :]], axis=1)
    node_hits = (conn[:, :, None] == jnp.arange(ext_nodes, dtype=jnp.int32)[None, None, :]).astype(
        jnp.float32
    )
    values = jnp.einsum("rn,kpn->rkp", extended, node_hits, precision=PRECISE)
    elem_u = values[:3].transpose(1, 0, 2).reshape(24, pt_dev)
    elem_v = values[3:].transpose(1, 0, 2).reshape(24, pt_dev)
    strain = jnp.einsum("ijp,jp->ip", strain_disp, elem_u, precision=PRECISE)
    dstrain = jnp.einsum("ijp,jp->ip", strain_disp, elem_v, precision=PRECISE)
    all_strains = whole_of(strain, DEV, 1)
    me_dev = lax.axis_index(DEV)
    grp_index = lax.axis_index("grp")
    mine = owner[:, 0] == me_dev
    rank = jnp.cumsum(mine.astype(jnp.int32)) - 1
    slot_ids = jnp.arange(slots, dtype=jnp.int32)
    select = ((rank[None, :] == slot_ids[:, None]) & mine[None, :]).astype(jnp.float32)
    own_strain = jnp.dot(all_strains, select.T, precision=PRECISE)
    own_count = jnp.sum(jnp.where(select > 0.0, counts[None, :], 0), axis=1)
    live = jnp.sum(mine.astype(jnp.int32))
    point_numbers = jnp.arange(total_points, dtype=jnp.int32).astype(jnp.float32)
    ids = jnp.where(slot_ids < live, jnp.dot(select, point_numbers, precision=PRECISE), -1.0)
    pattern = phase[0]
    hard = pattern == 1
    params = (
        jnp.where(hard, KAPPA_MARTENSITE, KAPPA_FERRITE).astype(jnp.float32),
        jnp.where(hard, SHEAR_MARTENSITE, SHEAR_FERRITE).astype(jnp.float32),
        jnp.where(hard, SOFT_MARTENSITE, SOFT_FERRITE).astype(jnp.float32),
    )
    voxels = pattern.shape[0]
    edge = NV
    half = slots // 2
    paired_strain = own_strain.reshape(6, half, 2)
    paired_count = own_count.reshape(half, 2)
    first_core = grp_index == 0
    part_strain = jnp.where(first_core, paired_strain[:, :, 0], paired_strain[:, :, 1])
    part_count = jnp.where(first_core, paired_count[:, 0], paired_count[:, 1])
    part_live = (live + 1 - grp_index) // 2
    tables = dft_tables(edge)
    normal = directions(edge)
    results = jnp.zeros((27, part_strain.shape[1]), jnp.float32)

    def run_point(slot, acc):
        mean_strain = lax.dynamic_slice_in_dim(part_strain, slot, 1, 1)
        start_field = jnp.broadcast_to(mean_strain, (6, voxels))
        final = lax.fori_loop(
            0,
            part_count[slot],
            lambda step, state: spectral_step(state, params, tables, normal),
            start_field,
        )
        return lax.dynamic_update_slice_in_dim(acc, summarize(final, params)[:, None], slot, 1)

    solved = lax.fori_loop(0, part_live, run_point, results)
    blank = jnp.zeros_like(solved)
    own_results = jnp.where(
        first_core, jnp.stack([solved, blank], axis=2), jnp.stack([blank, solved], axis=2)
    ).reshape(27, slots)
    gathered, gathered_ids = (whole_of(own_results, DEV, 1), whole_of(ids[None, :], DEV, 1))
    local_ids = (me_dev * pt_dev + jnp.arange(pt_dev, dtype=jnp.int32)).astype(jnp.float32)
    pick = (gathered_ids[0][:, None] == local_ids[None, :]).astype(jnp.float32)
    part_results = jnp.dot(gathered, pick, precision=PRECISE)
    results = total_of_pieces(part_results, "grp")
    point_stress = results[:6]
    tangent = results[jnp.asarray(tangent_table())]
    images = jnp.einsum("ijp,jp->ip", tangent, dstrain, precision=PRECISE)
    force_terms = jnp.einsum("ikp,ip->kp", strain_disp, point_stress, precision=PRECISE)
    image_terms = jnp.einsum("ikp,ip->kp", strain_disp, images, precision=PRECISE)
    force_terms = force_terms.reshape(8, 3, pt_dev).transpose(1, 0, 2)
    image_terms = image_terms.reshape(8, 3, pt_dev).transpose(1, 0, 2)
    terms = jnp.concatenate([force_terms, image_terms], axis=0)
    acc = jnp.einsum("rkp,kpn->rn", terms, node_hits, precision=PRECISE)
    returned = padded(acc[:, node_dev:], ((DEV, 1),), span)
    folded = jnp.concatenate([returned[:, :span], returned[:, 3 * span :]], axis=1)
    own = acc[:, :node_dev] + jnp.dot(folded, row_hits, precision=PRECISE)
    return (point_stress, own[:3], own[3:])


def solution(mesh):
    finer = Mesh(
        mesh.devices.reshape(mesh.shape["grp"], 8, 4, 4), ("grp", "dev_0", "dev_1", "dev_2")
    )
    return jax.shard_map(
        on_device,
        mesh=finer,
        in_specs=(
            P(None, DEV),
            P(None, DEV),
            P(None, None, DEV),
            P(None, DEV),
            P(DEV),
            P(),
            P(),
            P(DEV, None),
        ),
        out_specs=(P(None, DEV), P(None, DEV), P(None, DEV)),
        check_vma=False,
    )
```

profile of v0, /device:TPU:1, one launch (start us, length us, event | category | flops | bytes accessed | tf_op | source)
XLA Modules:
  0.0 882.1 jit_solution(16175561331352395232)
XLA Ops:
  1.5 4.0 collective-permute-start
  15.9 9.5 %all-reduce.2 = f32[32]{0:T(128)S(1)} all-reduce(f32[32]{0:T(128)S(1)} %dynamic-update-slice), channel_id=2, replica_groups=mesh['grp'=2,'dev_0'=8,'dev_1'=4,'dev_2'=4] {'dev_2'}, use_global_device_ids=true, to_apply=%add.2 | all-reduce | flops 32 | bytes 256
  27.6 8.4 all-reduce.3
  36.0 15.5 %all-gather.6 = f32[8,1,128]{2,1,0:T(1,128)} all-gather(f32[1,1,128]{2,1,0:T(1,128)S(1)} %bitcast.576), channel_id=4, replica_groups=mesh['grp'=2,'dev_0'=8,'dev_1'=4,'dev_2'=4] {'dev_0'}, dimensions={0}, use_global_device_ids=true | all-gather | bytes 4608 | tf_op jit(solution)/shard_map/all_gather | solution.py:45
  56.2 6.2 all-gather.4
  62.5 9.0 %all_gather.34 = f32[6,32]{0,1:T(8,128)S(1)} all-gather(f32[6,8]{0,1:T(8,128)S(1)} %bitcast.562), channel_id=1, replica_groups=mesh['grp'=2,'dev_0'=8,'dev_1'=4,'dev_2'=4] {'dev_1'}, dimensions={1}, use_global_device_ids=true | all-gather | bytes 960 | tf_op jit(solution)/shard_map/all_gather | solution.py:45
  71.6 18.1 %all-gather.5 = f32[8,32,6]{1,2,0:T(8,128)S(1)} all-gather(f32[1,32,6]{1,2,0:T(8,128)S(1)} %copy.130), channel_id=1, replica_groups=mesh['grp'=2,'dev_0'=8,'dev_1'=4,'dev_2'=4] {'dev_0'}, dimensions={0}, use_global_device_ids=true | all-gather | bytes 6912 | tf_op jit(solution)/shard_map/all_gather | solution.py:45
  91.0 356.4 %while.50 = (s32[]{:T(128)}, f32[27,4]{0,1:T(4,128)}, s32[]{:T(128)}, f32[32768]{0:T(1024)S(1)}, f32[6,4]{0,1:T(4,128)}, /*index=5*/s32[4]{0:T(128)S(1)}, f32[32...) while((s32[]{:T(128)}, f32[27,4]{0,1:T(4,128)}, ...), condition=%wide.region_12.13_spmd.clone.clone.clone, body=%wide.region_5.12_spmd.sunk.clone.clone.clone.sunk | while | flops 1546107264 | bytes 140536048 | solution.py:235
  94.6 326.8 %while.51 = (s32[]{:T(128)}, f32[6,32768]{1,0:T(8,128)S(1)}, s32[]{:T(128)}, f32[32768]{0:T(1024)}, f32[32768]{0:T(1024)S(1)}, /*index=5*/f32[32768]{0:T(1024)},...) while((s32[]{:T(128)}, f32[6,32768]{1,0:T(8,128)S(1)}, ...), condition=%wide.wide.region_8.8_spmd.clone.clone, body=%wide.wide.region_6.7_spmd.sunk.clone.clone.sunk | while | flops 1525317632 | bytes 131875360 | solution.py:227
  103.5 4.8 copy.197
  117.2 4.3 copy.196
  130.6 4.3 copy.199
  146.8 4.3 copy.198
  193.5 4.3 copy.205
  209.0 4.5 copy.204
  222.6 4.3 copy.207
  236.3 4.3 copy.206
  248.4 4.0 copy.208
  264.9 4.6 copy.197
  278.4 4.3 copy.196
  291.8 4.3 copy.199
  307.5 4.3 copy.198
  354.5 4.3 copy.205
  370.0 4.4 copy.204
  383.5 4.3 copy.207
  397.3 4.3 copy.206
  409.3 4.0 copy.208
  429.8 13.3 %concatenate.34 = f32[27]{0:T(128)S(1)} concatenate(f32[6]{0:T(128)S(1)} %broadcast_multiply_fusion.8, f32[1]{0:T(128)} %bitcast.435, f32[1]{0:T(128)} %bitcast.436, f32[1]{0:T(128)} %bitcast.437, f32[1]{0:T(128)} %bitcast.438, f32[1]{0:T(128)} %bitcast.439, f32[1]{0:T(128)} %bitcast.440, f32[1]{0:T(128)} %bitcast.441, f32[1]{0:T(128)} %bitcast.442, f32[1]{0:T(128)} %bitcast.443, ...), dimensions={0} | concatenate | bytes 216 | tf_op jit(solution)/shard_map/while/body/concatenate | solution.py:167
  448.2 9.0 %all_gather.36 = f32[27,32]{0,1:T(8,128)S(1)} all-gather(f32[27,8]{0,1:T(8,128)S(1)} %bitcast.565), channel_id=1, replica_groups=mesh['grp'=2,'dev_0'=8,'dev_1'=4,'dev_2'=4] {'dev_2'}, dimensions={1}, use_global_device_ids=true | all-gather | bytes 4320 | tf_op jit(solution)/shard_map/all_gather | solution.py:45
  457.3 9.0 %all_gather.37 = f32[27,128]{0,1:T(8,128)S(1)} all-gather(f32[27,32]{0,1:T(8,128)S(1)} %all_gather.36), channel_id=1, replica_groups=mesh['grp'=2,'dev_0'=8,'dev_1'=4,'dev_2'=4] {'dev_1'}, dimensions={1}, use_global_device_ids=true | all-gather | bytes 17280 | tf_op jit(solution)/shard_map/all_gather | solution.py:45
  466.2 19.1 %all_gather.38 = f32[27,1024]{0,1:T(8,128)S(1)} all-gather(f32[27,128]{0,1:T(8,128)S(1)} %all_gather.37), channel_id=1, replica_groups=mesh['grp'=2,'dev_0'=8,'dev_1'=4,'dev_2'=4] {'dev_0'}, dimensions={1}, use_global_device_ids=true | all-gather | bytes 124416 | tf_op jit(solution)/shard_map/all_gather | solution.py:45
  486.7 382.5 %all-gather.7 = f32[2,27,2]{1,2,0:T(2,128)S(1)} all-gather(f32[1,27,2]{1,2,0:T(2,128)S(1)} %convolution_bitcast_fusion.4), channel_id=5, replica_groups=mesh['grp'=2,'dev_0'=8,'dev_1'=4,'dev_2'=4] {'grp'}, dimensions={0}, use_global_device_ids=true | all-gather | bytes 648 | tf_op jit(solution)/shard_map/all_gather | solution.py:50
  (292 shorter events, 285.4 us)
Async XLA Ops:
  0.6 55.5 %copy-start = (f32[6,24,2]{1,2,0:T(2,128)S(1)}, f32[6,24,2]{1,2,0:T(2,128)}, u32[]{:S(2)}) copy-start(f32[6,24,2]{1,2,0:T(2,128)} %param.18) | copy-start | bytes 3460
  1.5 52.7 %collective-permute-start = (f32[6,1]{0,1:T(1,128)S(1)}, f32[6,1]{0,1:T(1,128)S(1)}, u32[]{:S(2)}, u32[]{:S(2)}) collective-permute-start(f32[6,1]{0,1:T(1,128)S(1)} %get-tuple-element.1508), channel_id=1, source_target_pairs={{0,1},{1,2},{2,3},{3,4},{4,5},{5,6},{6,7},{7,8},{8,9},{9,10},{10,1... | collective-permute-start | bytes 80 | tf_op jit(solution)/shard_map/ppermute | solution.py:36
  5.6 48.7 %collective-permute-start.1 = (f32[6,1]{0,1:T(1,128)S(1)}, f32[6,1]{0,1:T(1,128)S(1)}, u32[]{:S(2)}, u32[]{:S(2)}) collective-permute-start(f32[6,1]{0,1:T(1,128)S(1)} %get-tuple-element.1509), channel_id=1, source_target_pairs={{1,0},{2,1},{3,2},{4,3},{5,4},{6,5},{7,6},{8,7},{9,8},{10,9},{11,1... | collective-permute-start | bytes 80 | tf_op jit(solution)/shard_map/ppermute | solution.py:37
  91.0 394.3 %copy-start.18 = (f32[8,1,128]{2,1,0:T(1,128)S(1)}, f32[8,1,128]{2,1,0:T(1,128)}, u32[]{:S(2)}) copy-start(f32[8,1,128]{2,1,0:T(1,128)} %all-gather.6) | copy-start | bytes 12292
  91.0 778.2 %copy-start.17 = (s32[1024]{0:T(1024)S(1)}, s32[1024]{0:T(1024)}, u32[]{:S(2)}) copy-start(s32[1024]{0:T(1024)} %pad_clamp_fusion) | copy-start | bytes 12292
  95.6 4.3 copy-start.9
  95.6 15.7 %copy-start.7 = (f32[32,32]{1,0:T(8,128)}, f32[32,32]{1,0:T(8,128)S(1)}, u32[]{:S(2)}) copy-start(f32[32,32]{1,0:T(8,128)S(1)} %get-tuple-element.1916) | copy-start | bytes 12292 | tf_op jit(solution)/shard_map/while/body/while
  121.5 3.2 copy-start.5
  151.0 3.2 copy-start.3
  178.7 5.6 copy-start.1
  178.7 5.7 copy-start.2
  213.4 3.2 copy-start.4
  240.6 3.5 copy-start.10
  240.6 4.3 copy-start.6
  240.6 4.3 copy-start.8
  252.4 3.5 copy-start.12
  257.0 4.3 copy-start.9
  257.0 15.5 %copy-start.7 = (f32[32,32]{1,0:T(8,128)}, f32[32,32]{1,0:T(8,128)S(1)}, u32[]{:S(2)}) copy-start(f32[32,32]{1,0:T(8,128)S(1)} %get-tuple-element.1916) | copy-start | bytes 12292 | tf_op jit(solution)/shard_map/while/body/while
  282.7 3.2 copy-start.5
  311.8 3.2 copy-start.3
  339.7 5.6 copy-start.1
  339.7 5.7 copy-start.2
  374.4 3.2 copy-start.4
  401.5 3.4 copy-start.10
  401.6 4.2 copy-start.6
  401.6 4.2 copy-start.8
  413.3 3.5 copy-start.12
  421.4 4.0 copy-start.16
  421.9 22.5 %copy-start.21 = (s32[4]{0:T(128)S(1)}, s32[4]{0:T(128)}, u32[]{:S(2)}) copy-start(s32[4]{0:T(128)} %copy-done.20) | copy-start | bytes 52 | tf_op jit(solution)/shard_map/while
  869.2 12.5 %copy-start.19 = (f32[27,2]{0,1:T(2,128)}, f32[27,2]{0,1:T(2,128)S(1)}, u32[]{:S(2)}) copy-start(f32[27,2]{0,1:T(2,128)S(1)} %reduce_sum.96) | copy-start | bytes 652
  872.6 3.8 collective-permute-start.2
  875.1 4.3 collective-permute-start.3
  (6 other events, 6.9 us)
where the time goes:
time: 895 us; the launch traced here: 882 us
  blocking collectives  486 us (54%)
  local copies, waits for them, and re-layouts  255 us (28%)
  matrix products  76.4 us (9%)
  other arithmetic  36.8 us (4%)
  loops' own time  11.8 us (1%)
  starting transfers between devices  9.06 us (1%)
    all_gather x1, blocking collectives, total_of_pieces(): pieces = lax.all_gather(array, axis)  382 us
    reshape x52, local copies, waits for them, and re-layouts, rotate(): matrix.reshape(edge, 6, edge, edge).transpose(2, 1, 3, 0).reshape(edge, -1)  181 us
    all_gather x7, blocking collectives, whole_of(): nearer = lax.all_gather(array, axes[-1], axis=dim, tiled=True)  86 us
    div x6, local copies, waits for them, and re-layouts, spectral_step(): return field - spatial / field.shape[1]  19.8 us
    dot_general x10, matrix products, axis_pass(): sin_real = jnp.dot(sin_t, real, precision=PRECISE)  19.1 us
    unnamed x2, blocking collectives  17.9 us
  transfers between devices with their start and end apart: 4, of which 1 were waited for; matrix products, arithmetic and copies ran while one was open for 1% of the time, Pallas kernels for 0%

commit v1 on v0

v1 whole, which is shorter than its diff:
```python
import functools

import jax
import jax.numpy as jnp
import ml_dtypes
import numpy as np
from jax import lax
from jax.experimental import pallas as pl
from jax.experimental.pallas import tpu as pltpu
from jax.sharding import PartitionSpec as P

MERGED = False

EXACT = lax.Precision.HIGHEST
F32 = jnp.float32
BF16 = jnp.bfloat16
MESH = pl.DeviceIdType.MESH
VOXELS = 32768
ROOT_TWO = 1.4142135623730951
KAPPA = (2.0, 2.4)
SHEAR = (1.0, 1.3)
SOFT = (0.4, 2.5)
KAPPA_MEDIUM = 2.2
SHEAR_MEDIUM = 0.75
LAME_MEDIUM = KAPPA_MEDIUM - 2.0 * SHEAR_MEDIUM / 3.0
COUPLING = (LAME_MEDIUM + SHEAR_MEDIUM) / (LAME_MEDIUM + 2.0 * SHEAR_MEDIUM)
UPPER = [(i, j) for i in range(6) for j in range(i, 6)]
NONE = 4096.0


def two_parts(table):
    high = table.astype(np.float32).astype(ml_dtypes.bfloat16)
    low = (table - high.astype(np.float64)).astype(np.float32).astype(ml_dtypes.bfloat16)
    return high, low


def dft_tables():
    n32, n8, n4 = np.arange(32), np.arange(8), np.arange(4)
    f32 = np.exp(-2j * np.pi / 32 * np.outer(n32, n32))
    f8 = np.exp(-2j * np.pi / 8 * np.outer(n8, n8))
    f4 = np.exp(-2j * np.pi / 4 * np.outer(n4, n4))
    left = np.einsum("ab,cd->cabd", f32, f8).reshape(256, 256)
    left = np.block([[left.real, -left.imag], [left.imag, left.real]])
    rights = []
    for k0 in range(8):
        turn = np.exp(-2j * np.pi / 32 * n4 * k0)[:, None] * f4
        one = np.einsum("ab,cd->acbd", turn, f32).reshape(128, 128)
        rights.append(np.block([[one.real, one.imag], [-one.imag, one.real]]))
    right = np.stack(rights)
    return left, right, left.T / VOXELS, right.transpose(0, 2, 1)


def green_tables():
    row, lane = np.arange(256)[:, None], np.arange(128)[None, :]
    k = [row % 32 + 0 * lane, 8 * (lane // 32) + row // 32, lane % 32 + 0 * row]
    freq = [np.where(v < 16, v, v - 32).astype(np.float64) for v in k]
    length = np.sqrt(np.maximum(sum(f * f for f in freq), 1.0))
    normal = [f / length for f in freq]
    edge = [v == 16 for v in k]
    pairs = [(0, 0), (1, 1), (2, 2), (1, 2), (0, 2), (0, 1)]
    both = [
        normal[i] * normal[j] * (1.0 if i == j else ROOT_TWO) / SHEAR_MEDIUM for i, j in pairs
    ]
    even = [np.where(edge[i] == edge[j], v, 0.0) for (i, j), v in zip(pairs, both)]
    odd = [np.where(edge[i] == edge[j], 0.0, v) for (i, j), v in zip(pairs, both)][3:]
    return np.stack(even + odd).astype(np.float32)


def message_tables():
    spread = np.zeros((2, 2, 128, 128), np.float32)
    for uv in range(2):
        for d in range(3):
            for j in range(12):
                spread[uv, 0, 16 * d + 12 + uv, 32 + 16 * d + j] = 1.0
                spread[uv, 1, 16 * d + 14 + uv, 80 + 16 * d + j] = 1.0
    splat = np.zeros((128, 6, 128), np.float32)
    expand = np.zeros((128, 128), np.float32)
    for g in range(8):
        for i in range(6):
            for p in range(2):
                splat[16 * g + 2 * i + p, i, :] = 1.0
                for k in range(6):
                    expand[16 * g + 2 * i + p, 8 + 6 * i + k] = 1.0
    deal = np.zeros((2, 128, 128), np.float32)
    for i in range(6):
        for p in range(2):
            for lead in [0] + [32 + 16 * g for g in range(6)]:
                deal[0, i, lead + 2 * i + p] = 1.0
                for j in range(6):
                    deal[1, 8 + 6 * j + i, lead + 2 * i + p] = 1.0
    pack = lambda a: a.transpose(1, 0, 2).reshape(128, -1)
    return pack(spread[0]), splat.reshape(128, 768), pack(spread[1]), expand, pack(deal)


def summary_table():
    table = np.zeros((2, 32, 8, 128), np.float64)
    unit = np.array([1.0, 1, 1, 0, 0, 0])
    outer = np.outer(unit, unit)
    project = np.eye(6) - outer / 3.0
    for q in range(2):
        for i in range(6):
            table[q, 0, :, 64 * q + i] = unit[i]
            table[q, 1 + i, :, 64 * q + i] = 1.0
            for j in range(6):
                lane = 64 * q + 8 + 6 * j + i
                table[q, 29, :, lane] = outer[i, j]
                table[q, 7, :, lane] = 2.0 * project[i, j]
                place = UPPER.index((min(i, j), max(i, j)))
                table[q, 8 + place, :, lane] = -1.0
    return (table.reshape(512, 128) / VOXELS).astype(np.float32)


def iota(shape, dim):
    return lax.broadcasted_iota(jnp.int32, shape, dim)


def lanes_f32():
    return iota((8, 128), 1).astype(F32)


def exact_dot(a, b):
    return jnp.dot(a, b, precision=EXACT, preferred_element_type=F32)


def split(value):
    high = value.astype(BF16)
    return high, (value - high.astype(F32)).astype(BF16)


def dot3(a_high, a_low, b_high, b_low):
    out = jnp.dot(a_high, b_high, preferred_element_type=F32)
    out = out + jnp.dot(a_low, b_high, preferred_element_type=F32)
    return out + jnp.dot(a_high, b_low, preferred_element_type=F32)


def plane_peer(other):
    dev = lax.axis_index("dev")
    return (dev // 16) * 16 + (dev + other) % 16


def column_peer(other):
    return (lax.axis_index("dev") + 16 * other) % 128


def greet(both_cores):
    barrier = pltpu.get_barrier_semaphore()
    grp = lax.axis_index("grp")
    peers = [(grp, plane_peer(j)) for j in range(1, 16)]
    peers += [(grp, column_peer(j)) for j in range(1, 8)]
    if both_cores:
        peers += [((grp + 1) % 2, plane_peer(j)) for j in range(16)]
    for peer in peers:
        pl.semaphore_signal(barrier, inc=1, device_id=peer, device_id_type=MESH)
    pl.semaphore_wait(barrier, len(peers))


def copy_to(src, dst, send, recv, peer):
    return pltpu.make_async_remote_copy(
        src_ref=src, dst_ref=dst, send_sem=send, recv_sem=recv,
        device_id=peer, device_id_type=MESH,
    )


def gather_start(rows, row, cores, sems):
    dev, grp = lax.axis_index("dev"), lax.axis_index("grp")
    level = dev // 16
    mine = dev % 16 + (16 * grp if cores == 2 else 0)
    rows[level, pl.ds(mine, 1), :] = row
    copies = []
    for core in range(cores):
        for j in range(1 - core, 16):
            peer = ((grp + core) % 2, plane_peer(j))
            n = 16 * core + j
            here = rows.at[level, pl.ds(mine, 1)]
            copies.append(copy_to(here, here, sems[0].at[n], sems[1].at[n], peer))
    for copy in copies:
        copy.start()
    return copies


def gather_across(rows, sems):
    level, grp = lax.axis_index("dev") // 16, lax.axis_index("grp")
    here = rows.at[level]
    copies = [
        copy_to(here, here, sems[2].at[j], sems[3].at[j], (grp, column_peer(j)))
        for j in range(1, 8)
    ]
    for copy in copies:
        copy.start()
    return copies


def wait_all(copies):
    for copy in copies:
        copy.wait()


def widened(b_ref, conn_ref, d):
    del conn_ref
    parts = [b_ref[i, pl.ds(d, 8, stride=3), :] for i in range(6)]
    parts.append(jnp.zeros((8, 116), F32))
    return jnp.concatenate(parts, axis=1)


def partition_row(disp, probe, b_ref, conn_ref, listed, near_ref):
    lane, sub = iota((8, 128), 1), iota((8, 128), 0)
    conn = conn_ref[...]
    conn = jnp.concatenate([conn] * 6 + [jnp.full((8, 116), -1, jnp.int32)], axis=1)
    weights = [widened(b_ref, conn_ref, d) for d in range(3)]
    total = jnp.zeros((8, 128), F32)
    for uv, field in enumerate((disp, probe)):
        base = jnp.zeros((8, 128), F32)
        for d in range(3):
            value = jnp.zeros((8, 128), F32)
            for n in range(4):
                value = jnp.where(conn == n, field[d, n], value)
            base = base + weights[d] * value
        total = total + (pltpu.roll(base, 16, 1) if uv else base)
    for end in range(2):
        for d in range(3):
            one = jnp.where(conn == 4 + end, weights[d], 0.0)
            total = total + pltpu.roll(one, 32 + 48 * end + 16 * d, 1)
    row = jnp.sum(total, axis=0, keepdims=True)
    for d in range(3):
        for uv, field in enumerate((disp, probe)):
            for way in range(2):
                value = jnp.zeros((1, 128), F32)
                for n in range(4):
                    value = jnp.where(
                        jnp.full((1, 128), listed[1 - way], jnp.int32) == n, field[d, n], value
                    )
                row = jnp.where(lane[:1] == 16 * d + 12 + 2 * way + uv, value, row)
    for n in range(4):
        near = jnp.zeros((8, 128), F32)
        for d in range(3):
            one = jnp.sum(jnp.where(conn == n, weights[d], 0.0), axis=0, keepdims=True)
            near = jnp.where(sub == d, one, near)
        near_ref[n] = near
    return row


def point_rows(rows, point, uv, spread):
    lane = lanes_f32()
    part = jnp.floor(point * 0.5)
    parity = point - 2.0 * part
    pick = jnp.concatenate([lane == part, lane == part - 1.0, lane == part + 1.0], axis=0)
    found = exact_dot(pick.astype(F32), rows)
    below = exact_dot(found[8:16], spread[:, :128])
    above = exact_dot(found[16:24], spread[:, 128:])
    count = iota((8, 128), 1)
    base = ((count // 16) == uv).astype(F32)
    own = (count % 2).astype(F32) == parity
    factor = jnp.where((count % 16) < 12, base + below + above, 0.0)
    return found[:8], jnp.where(own, found[:8] * factor, 0.0)


def my_points(owner, counts):
    me, grp = lax.axis_index("dev"), lax.axis_index("grp")
    index = iota((1, 256), 1).astype(F32)
    mine = owner == me
    first = jnp.min(jnp.where(mine, index, NONE), axis=1, keepdims=True)
    second = jnp.min(jnp.where(mine & (index > first), index, NONE), axis=1, keepdims=True)
    third = jnp.min(jnp.where(mine & (index > second), index, NONE), axis=1, keepdims=True)
    even = jnp.full((1, 1), grp, jnp.int32) == 0
    slots = (jnp.where(even, first, second), jnp.where(even, third, NONE))
    sub = iota((8, 128), 0)
    point = jnp.where(sub == 0, slots[0], jnp.where(sub == 1, slots[1], NONE))
    turns = [
        jnp.sum(jnp.where(index == slot, counts.astype(F32), 0.0), axis=1, keepdims=True)
        for slot in slots
    ]
    return point, turns


def green(tau, t, odd):
    half = [0.5 * t[q] for q in (3, 4, 5)]
    cross = [v * (1.0 / ROOT_TWO) for v in half]
    p3, p4, p5 = (half[0] * tau[3], half[1] * tau[4], half[2] * tau[5])
    d0, d1, d2 = (t[0] * tau[0], t[1] * tau[1], t[2] * tau[2])
    along = (COUPLING * SHEAR_MEDIUM) * (d0 + d1 + d2 + 2.0 * (p3 + p4 + p5))
    aside = (COUPLING * SHEAR_MEDIUM) * (odd[0] * tau[3] + odd[1] * tau[4] + odd[2] * tau[5])
    s12, s02, s01 = (0.5 * (t[1] + t[2]), 0.5 * (t[0] + t[2]), 0.5 * (t[0] + t[1]))
    return [
        d0 + p5 + p4 - along * t[0],
        d1 + p5 + p3 - along * t[1],
        d2 + p4 + p3 - along * t[2],
        cross[2] * tau[4] + cross[1] * tau[5] + half[0] * (tau[1] + tau[2]) + s12 * tau[3]
        - along * t[3] - aside * odd[0],
        cross[2] * tau[3] + cross[0] * tau[5] + half[1] * (tau[0] + tau[2]) + s02 * tau[4]
        - along * t[4] - aside * odd[1],
        cross[1] * tau[3] + cross[0] * tau[4] + half[2] * (tau[0] + tau[1]) + s01 * tau[5]
        - along * t[5] - aside * odd[2],
    ]


def law(e, kappa, shear, scale):
    trace = e[0] + e[1] + e[2]
    third = trace * (1.0 / 3.0)
    dev = [e[i] - third for i in range(3)] + list(e[3:])
    size = dev[0] * dev[0]
    for v in dev[1:]:
        size = size + v * v
    factor = lax.rsqrt(1.0 + size * scale)
    return kappa * trace, dev, 2.0 * shear * factor, factor


def by_phase(hard, pair):
    return jnp.where(hard, pair[1], pair[0])


def materials(hard):
    return (
        by_phase(hard, KAPPA), by_phase(hard, SHEAR),
        by_phase(hard, (1.0 / SOFT[0] ** 2, 1.0 / SOFT[1] ** 2)),
    )


def phase_spectrum(c):
    pattern = (c.phase[...] == 1).astype(F32).astype(BF16)
    z = jnp.dot(c.lf_h[:, :256], pattern, preferred_element_type=F32)
    z = z + jnp.dot(c.lf_l[:, :256], pattern, preferred_element_type=F32)
    for k in range(8):
        rows = jnp.concatenate([z[32 * k : 32 * k + 32], z[256 + 32 * k : 288 + 32 * k]], axis=1)
        high, low = split(rows)
        c.chi[pl.ds(32 * k, 32), :] = dot3(high, low, c.rf_h[k], c.rf_l[k])


def back_right(c, k):
    high, low = split(c.spec[...])
    w = dot3(high, low, c.ri_h[k], c.ri_l[k])
    high, low = split(w)
    for q in range(6):
        for part in range(2):
            at = (pl.ds(pl.multiple_of(256 * part + 32 * k, 32), 32), pl.ds(128 * q, 128))
            from_ = (slice(32 * q, 32 * q + 32), slice(128 * part, 128 * part + 128))
            c.x_h[at] = high[from_]
            c.x_l[at] = low[from_]


def left(c, high, low, out):
    for q in range(3):
        cols = pl.ds(256 * q, 256)
        out[:, cols] = dot3(high[...], low[...], c.x_h[:, cols], c.x_l[:, cols])


def solve(c, e, turns):
    jumps = []
    for q in range(2):
        ends = []
        for m in range(2):
            kt, dev, stiff, _ = law(e[q], KAPPA[m], SHEAR[m], 1.0 / SOFT[m] ** 2)
            ends.append([stiff * v + (kt if i < 3 else 0.0) for i, v in enumerate(dev)])
        jumps.append([b - a for a, b in zip(*ends)])

    def first(k, carry):
        for part in range(4):
            at = pl.multiple_of(32 * k + 8 * part, 8)
            t = [c.green[q, pl.ds(at, 8), :] for q in range(9)]
            real, imag = c.chi[pl.ds(at, 8), :128], c.chi[pl.ds(at, 8), 128:]
            one, two = green(jumps[0], t[:6], t[6:]), green(jumps[1], t[:6], t[6:])
            for q in range(6):
                rows = slice(32 * q + 8 * part, 32 * q + 8 * part + 8)
                c.spec[rows, :128] = real * one[q] - imag * two[q]
                c.spec[rows, 128:] = real * two[q] + imag * one[q]
        back_right(c, k)
        return carry

    lax.fori_loop(0, 8, first, 0)
    left(c, c.li_h, c.li_l, c.u)

    def stress(r, carry):
        at = pl.multiple_of(16 * r, 16)
        kappa, shear, scale = materials(c.phase[pl.ds(at, 16), :] == 1)
        for q in range(2):
            rows = pl.ds(pl.multiple_of(256 * q + 16 * r, 16), 16)
            field = [
                jnp.concatenate([e[q][i]] * 2, axis=0) - c.u[rows, pl.ds(128 * i, 128)]
                for i in range(6)
            ]
            kt, dev, stiff, _ = law(field, kappa, shear, scale)
            for i in range(6):
                c.f[rows, pl.ds(128 * i, 128)] = field[i]
                high, low = split(stiff * dev[i] + (kt if i < 3 else 0.0))
                c.x_h[rows, pl.ds(128 * i, 128)] = high
                c.x_l[rows, pl.ds(128 * i, 128)] = low
        return carry

    lax.fori_loop(0, 16, stress, 0)
    left(c, c.lf_h, c.lf_l, c.u)

    def middle(k, carry):
        near, far = pl.multiple_of(32 * k, 32), pl.multiple_of(256 + 32 * k, 32)
        rows = jnp.concatenate(
            [
                jnp.concatenate(
                    [c.u[pl.ds(near, 32), pl.ds(128 * q, 128)], c.u[pl.ds(far, 32), pl.ds(128 * q, 128)]],
                    axis=1,
                )
                for q in range(6)
            ],
            axis=0,
        )
        high, low = split(rows)
        c.spec[...] = dot3(high, low, c.rf_h[k], c.rf_l[k])
        for part in range(4):
            at = pl.multiple_of(32 * k + 8 * part, 8)
            t = [c.green[q, pl.ds(at, 8), :] for q in range(9)]
            for half in range(2):
                cols = slice(128 * half, 128 * half + 128)
                spots = [slice(32 * q + 8 * part, 32 * q + 8 * part + 8) for q in range(6)]
                out = green([c.spec[s, cols] for s in spots], t[:6], t[6:])
                for s, v in zip(spots, out):
                    c.spec[s, cols] = v
        back_right(c, k)
        return carry

    lax.fori_loop(0, 8, middle, 0)
    left(c, c.li_h, c.li_l, c.u)

    for q in range(2):
        keep = jnp.broadcast_to((turns[q] > 1.5).astype(F32), (8, 128))

        def total(r, sums, q=q, keep=keep):
            at = pl.multiple_of(8 * r, 8)
            kappa, shear, scale = materials(c.phase[pl.ds(at, 8), :] == 1)
            rows = pl.ds(pl.multiple_of(256 * q + 8 * r, 8), 8)
            field = [
                c.f[rows, pl.ds(128 * i, 128)] - keep * c.u[rows, pl.ds(128 * i, 128)]
                for i in range(6)
            ]
            kt, dev, stiff, factor = law(field, kappa, shear, scale)
            weight = stiff * factor * factor * scale
            heavy = [weight * v for v in dev]
            new = [kt] + [stiff * v for v in dev] + [shear * factor]
            new += [heavy[i] * dev[j] for i, j in UPPER] + [kappa]
            return tuple(s + v for s, v in zip(sums, new))

        sums = lax.fori_loop(0, 32, total, (jnp.zeros((8, 128), F32),) * 30)
        for n, v in enumerate(sums):
            c.sums[pl.ds(256 * q + 8 * n, 8), :] = v
        c.sums[pl.ds(256 * q + 240, 16), :] = jnp.zeros((16, 128), F32)
    ones = jnp.ones((8, 128), F32)
    lanes = lax.dot_general(
        ones, c.sums[...], (((1,), (1,)), ((), ())), precision=EXACT, preferred_element_type=F32
    )
    return exact_dot(lanes, c.summary[...])


def finish(rows, results, owner, listed, near, c, stress_ref, force_ref, image_ref):
    dev = lax.axis_index("dev")
    sub, lane = iota((8, 128), 0), iota((8, 128), 1)
    step = jnp.where(sub < 2, 0, jnp.where(sub < 4, -1, 1))
    point = (2 * (jnp.full((8, 128), dev, jnp.int32) + step) + sub % 2).astype(F32)
    point = jnp.where(sub < 6, point, NONE)
    found, masked = point_rows(rows, point, 1, c.spread_v[...])
    direction = exact_dot(masked, c.expand[...])
    index = iota((8, 256), 1).astype(F32)
    wide = jnp.concatenate([point, point], axis=1)
    owners = jnp.broadcast_to(owner.astype(F32), (8, 256))
    who = jnp.sum(jnp.where(index == wide, owners, 0.0), axis=1, keepdims=True)
    rank = jnp.sum(
        jnp.where((owners == who) & (index < wide), 1.0, 0.0), axis=1, keepdims=True
    )
    slot = jnp.floor(rank * 0.5)
    level = jnp.floor(who * 0.0625)
    place = who + 16.0 * level + 16.0 * (rank - 2.0 * slot)
    value = exact_dot((index == place).astype(F32), results)
    value = jnp.where(slot > 0.5, pltpu.roll(value, 64, 1), value)
    value = jnp.where(lane < 64, value, 0.0)
    terms = value * jnp.where(lane < 6, 1.0, direction)
    dealt = exact_dot(terms, c.deal[...])
    own_lane = lane % 2 == sub % 2
    out_sub, out_lane = sub, lane
    column = jnp.where(out_lane == 0, value[0:1], 0.0)
    del column
    picks = [
        jnp.sum(jnp.where(out_lane == out_sub, value[p : p + 1], 0.0), axis=1, keepdims=True)
        for p in range(2)
    ]
    stress_ref[...] = jnp.where(out_lane == 0, picks[0], picks[1])[:6, :2]
    for half, ref in enumerate((force_ref, image_ref)):
        y = jnp.where(own_lane, dealt[:, 128 * half : 128 * half + 128], 0.0)
        mine = jnp.sum(jnp.where(sub < 2, y, 0.0), axis=0, keepdims=True)
        linked = y * found
        before = jnp.sum(jnp.where((sub == 2) | (sub == 3), linked, 0.0), axis=0, keepdims=True)
        after = jnp.sum(jnp.where((sub == 4) | (sub == 5), linked, 0.0), axis=0, keepdims=True)
        twelve = lane % 16 < 12
        out = jnp.zeros((8, 128), F32)
        for n in range(4):
            got = jnp.sum(near[n] * mine, axis=1, keepdims=True)
            out = jnp.where(lane == n, got, out)
        for end, row, lead in ((0, before, 5), (1, after, 2)):
            part = jnp.where(twelve & (lane // 16 == sub + lead) & (sub < 3), row, 0.0)
            got = jnp.sum(part, axis=1, keepdims=True)
            out = out + jnp.where(lane == listed[end], got, 0.0)
        ref[...] = out[:3, :4]


TABLES = ("lf_h", "lf_l", "li_h", "li_l", "rf_h", "rf_l", "ri_h", "ri_l", "green")
SMALL = ("spread_u", "splat", "summary", "spread_v", "expand", "deal")
WORK = {
    "chi": ((256, 256), F32),
    "spec": ((192, 256), F32),
    "x_h": ((512, 768), BF16),
    "x_l": ((512, 768), BF16),
    "u": ((512, 768), F32),
    "f": ((512, 768), F32),
    "sums": ((512, 128), F32),
}


class Bag:
    def __init__(self, **refs):
        self.__dict__.update(refs)


def constants():
    lf, rf, li, ri = dft_tables()
    out = {"green": green_tables(), "summary": summary_table()}
    for name, table in (("lf", lf), ("li", li), ("rf", rf), ("ri", ri)):
        out[name + "_h"], out[name + "_l"] = two_parts(table)
    names = ("spread_u", "splat", "spread_v", "expand", "deal")
    out.update(zip(names, message_tables()))
    return out


def splats(rows, owner, counts, c):
    point, turns = my_points(owner, counts)
    _, masked = point_rows(rows, point, 0, c.spread_u[...])
    strain = exact_dot(masked, c.splat[...])
    e = [
        [jnp.broadcast_to(strain[q : q + 1, 128 * i : 128 * i + 128], (8, 128)) for i in range(6)]
        for q in range(2)
    ]
    return e, turns


VM = pl.BlockSpec(memory_space=pltpu.VMEM)
SM = pl.BlockSpec(memory_space=pltpu.SMEM)
SEMS = [
    pltpu.SemaphoreType.DMA((32,)), pltpu.SemaphoreType.DMA((32,)),
    pltpu.SemaphoreType.DMA((8,)), pltpu.SemaphoreType.DMA((8,)),
]


def first_kernel(disp, probe, b, conn, listed, rows_out, near_out, rows, *sems):
    row = partition_row(disp, probe, b, conn, listed, near_out)
    greet(False)
    wait_all(gather_start(rows, row, 1, sems))
    wait_all(gather_across(rows, sems))
    rows_out[...] = rows[...]


def second_kernel(names, *refs):
    c = Bag(**dict(zip(names, refs)))
    phase_spectrum(c)
    e, turns = splats(c.rows[...], c.owner[...], c.counts[...], c)
    c.out[...] = solve(c, e, turns)


def third_kernel(result, gathered, owner, listed, near, sv, ex, de, s_out, f_out, i_out, rows, *sems):
    c = Bag(spread_v=sv, expand=ex, deal=de)
    greet(True)
    wait_all(gather_start(rows, result[0:1, :], 2, sems))
    wait_all(gather_across(rows, sems))
    results = rows[...].reshape(256, 128)
    finish(gathered[...], results, owner[...], listed, near, c, s_out, f_out, i_out)


def on_device(disp, probe, strain_disp, conn, halo_rows, owner, counts, phase):
    table = {k: jnp.asarray(v) for k, v in constants().items()}
    owner, counts = owner.reshape(1, 256), counts.reshape(1, 256)
    phase = phase.reshape(256, 128)
    shape = jax.ShapeDtypeStruct
    rows, near = pl.pallas_call(
        first_kernel,
        out_shape=(shape((8, 16, 128), F32), shape((4, 8, 128), F32)),
        in_specs=[SM, SM, VM, VM, SM],
        out_specs=(VM, VM),
        scratch_shapes=[pltpu.VMEM((8, 16, 128), F32)] + SEMS,
        compiler_params=pltpu.CompilerParams(collective_id=0, has_side_effects=True),
    )(disp, probe, strain_disp, conn, halo_rows)
    rows = rows.reshape(128, 128)
    names = ("rows", "owner", "counts", "phase") + TABLES + SMALL[:3]
    args = [rows, owner, counts, phase] + [table[n] for n in TABLES + SMALL[:3]]
    result = pl.pallas_call(
        functools.partial(second_kernel, names + ("out",) + tuple(WORK)),
        out_shape=shape((8, 128), F32),
        in_specs=[VM] * len(args),
        out_specs=VM,
        scratch_shapes=[pltpu.VMEM(*v) for v in WORK.values()],
        compiler_params=pltpu.CompilerParams(vmem_limit_bytes=48 << 20),
    )(*args)
    outs = pl.pallas_call(
        third_kernel,
        out_shape=(shape((6, 2), F32), shape((3, 4), F32), shape((3, 4), F32)),
        in_specs=[VM, VM, VM, SM, VM, VM, VM, VM],
        out_specs=(VM, VM, VM),
        scratch_shapes=[pltpu.VMEM((8, 32, 128), F32)] + SEMS,
        compiler_params=pltpu.CompilerParams(collective_id=1, has_side_effects=True),
    )(result, rows, owner, halo_rows, near, *[table[n] for n in SMALL[3:]])
    return outs


def solution(mesh):
    dev = P(None, "dev")
    return jax.shard_map(
        on_device,
        mesh=mesh,
        in_specs=(dev, dev, P(None, None, "dev"), dev, P("dev"), P(), P(), P("dev", None)),
        out_specs=(dev, dev, dev),
        check_vma=False,
    )
```

time: 895 us -> 81.6 us (0.09); the launches traced: 882 us -> 80.8 us
  blocking collectives: 486 us -> 0 us
  local copies, waits for them, and re-layouts: 255 us -> 19.8 us
  matrix products: 76.4 us -> 0 us
  Pallas kernels: 0 us -> 60.4 us
  other arithmetic: 36.8 us -> 0 us
  loops' own time: 11.8 us -> 0 us
  starting transfers between devices: 9.06 us -> 0 us
    all_gather x8 -> x0, blocking collectives: 468 us -> none  [the longest x1 382 us: total_of_pieces(): pieces = lax.all_gather(array, axis)]
    reshape x63 -> x0, local copies, waits for them, and re-layouts: 182 us -> none  [the longest x52 181 us: rotate(): matrix.reshape(edge, 6, edge, edge).transpose(2, 1, 3, 0).reshape(edge, -1)]
    dot_general x53 -> x0, matrix products: 76.4 us -> none  [the longest x10 19.1 us: axis_pass(): sin_real = jnp.dot(sin_t, real, precision=PRECISE)]
    pallas_call x0 -> x3, Pallas kernels: none -> 60.4 us  [the longest x1 20.6 us: on_device(): pl.pallas_call(functools.partial(second_kernel, names + ('out',) + tuple(...]
    div x18 -> x0, local copies, waits for them, and re-layouts: 31 us -> none  [the longest x6 19.8 us: spectral_step(): return field - spatial / field.shape[1]]
    unnamed x2 -> x0, blocking collectives: 17.9 us -> none
    unnamed x18 -> x32, local copies, waits for them, and re-layouts: 4.52 us -> 18.4 us
    slice x4 -> x0, other arithmetic: 13.8 us -> none  [polarize(): tau[0] * first + tau[5] / ROOT_TWO * second + tau[4] / ROOT_TWO * third]
  transfers between devices with their start and end apart: 4 -> 0, of which waited for: 1 -> 0; matrix products, arithmetic and copies ran while one was open for 1% -> 0% of each run, Pallas kernels for 0% -> 0%
where the time goes in v1:
time: 81.6 us; the launch traced here: 80.8 us
  Pallas kernels  60.4 us (74%)
  local copies, waits for them, and re-layouts  19.8 us (24%)
    pallas_call x1, Pallas kernels, on_device(): pl.pallas_call(functools.partial(second_kernel, names + ('out',) + tuple(...  20.6 us
    pallas_call x1, Pallas kernels, on_device(): pl.pallas_call(third_kernel, out_shape=(shape((6, 2), F32), shape((3, 4),...  20.1 us
    pallas_call x1, Pallas kernels, on_device(): pl.pallas_call(first_kernel, out_shape=(shape((8, 16, 128), F32), shape((...  19.6 us
    unnamed x32, local copies, waits for them, and re-layouts  18.4 us

profile of v1, /device:TPU:1, one launch (start us, length us, event | category | flops | bytes accessed | tf_op | source)
XLA Modules:
  0.0 80.8 jit_solution(15025286148620358995)
XLA Ops:
  0.6 1.3 %copy.27.conn = s32[8,2]{1,0:T(8,128)} copy(s32[8,2]{0,1:T(2,128)} %param.26) | data formatting | bytes 128 | tf_op args[3]
  2.0 1.4 %copy.26.b = f32[6,24,2]{2,1,0:T(8,128)} copy(f32[6,24,2]{1,2,0:T(2,128)} %param.25) | data formatting | bytes 2304 | tf_op args[2]
  3.4 19.6 %shard_map.238 = (f32[8,16,128]{2,1,0:T(8,128)}, f32[4,8,128]{2,1,0:T(8,128)}) custom-call(f32[3,4]{1,0:T(4,128)} %disp.1, f32[3,4]{1,0:T(4,128)} %probe.1, f32[6,24,2]{2,1,0:T(8,128)} %copy.26.b, s32[8,2]{1,0:T(8,128)} %copy.27.conn, s32[2]{0:T(128)} %listed.3), custom_call_target="tpu_custom_call" | custom-call | tf_op jit(solution)/shard_map/pallas_call | solution.py:575
  23.0 0.0 copy-start
  23.0 1.2 %copy-done = bf16[8,256,256]{2,1,0:T(8,128)(2,1)S(1)} copy-done((bf16[8,256,256]{2,1,0:T(8,128)(2,1)S(1)}, bf16[8,256,256]{2,1,0:T(8,128)(2,1)}, u32[]{:S(2)}) %copy-start) | copy-done | bytes 1048600
  24.3 0.0 copy-start.1
  24.3 1.2 %copy-done.1 = bf16[8,256,256]{2,1,0:T(8,128)(2,1)S(1)} copy-done((bf16[8,256,256]{2,1,0:T(8,128)(2,1)S(1)}, bf16[8,256,256]{2,1,0:T(8,128)(2,1)}, u32[]{:S(2)}) %copy-start.1) | copy-done | bytes 1048600
  25.5 0.0 copy-start.2
  25.5 1.0 %copy-done.2 = bf16[512,512]{1,0:T(8,128)(2,1)S(1)} copy-done((bf16[512,512]{1,0:T(8,128)(2,1)S(1)}, bf16[512,512]{1,0:T(8,128)(2,1)}, u32[]{:S(2)}) %copy-start.2) | copy-done | bytes 524312
  26.5 0.0 copy-start.3
  26.5 1.0 %copy-done.3 = bf16[512,512]{1,0:T(8,128)(2,1)S(1)} copy-done((bf16[512,512]{1,0:T(8,128)(2,1)S(1)}, bf16[512,512]{1,0:T(8,128)(2,1)}, u32[]{:S(2)}) %copy-start.3) | copy-done | bytes 524312
  27.6 0.0 copy-start.4
  27.6 1.0 %copy-done.4 = bf16[512,512]{1,0:T(8,128)(2,1)S(1)} copy-done((bf16[512,512]{1,0:T(8,128)(2,1)S(1)}, bf16[512,512]{1,0:T(8,128)(2,1)}, u32[]{:S(2)}) %copy-start.4) | copy-done | bytes 524312
  28.6 0.0 copy-start.5
  28.6 1.0 %copy-done.5 = bf16[512,512]{1,0:T(8,128)(2,1)S(1)} copy-done((bf16[512,512]{1,0:T(8,128)(2,1)S(1)}, bf16[512,512]{1,0:T(8,128)(2,1)}, u32[]{:S(2)}) %copy-start.5) | copy-done | bytes 524312
  29.7 0.0 copy-start.6
  29.7 1.0 %copy-done.6 = f32[128,768]{1,0:T(8,128)S(1)} copy-done((f32[128,768]{1,0:T(8,128)S(1)}, f32[128,768]{1,0:T(8,128)}, u32[]{:S(2)}) %copy-start.6) | copy-done | bytes 393240
  30.7 0.0 copy-start.7
  30.7 0.8 %copy-done.7 = f32[8,16,128]{2,1,0:T(8,128)S(1)} copy-done((f32[8,16,128]{2,1,0:T(8,128)S(1)}, f32[8,16,128]{2,1,0:T(8,128)}, u32[]{:S(2)}) %copy-start.7) | copy-done | bytes 65560
  31.5 0.0 copy-start.8
  31.5 0.9 %copy-done.8 = f32[512,128]{1,0:T(8,128)S(1)} copy-done((f32[512,128]{1,0:T(8,128)S(1)}, f32[512,128]{1,0:T(8,128)}, u32[]{:S(2)}) %copy-start.8) | copy-done | bytes 262168
  32.4 0.0 copy-start.9
  32.4 0.9 %copy-done.9 = s32[1,32768]{1,0:T(1,128)S(1)} copy-done((s32[1,32768]{1,0:T(1,128)S(1)}, s32[1,32768]{1,0:T(1,128)}, u32[]{:S(2)}) %copy-start.9) | copy-done | bytes 131096
  33.3 0.9 %copy-done.10 = f32[128,256]{1,0:T(8,128)S(1)} copy-done((f32[128,256]{1,0:T(8,128)S(1)}, f32[128,256]{1,0:T(8,128)}, u32[]{:S(2)}) %copy-start.10) | copy-done | bytes 131096
  34.3 0.7 copy-done.12
  34.9 0.7 copy-done.13
  35.6 20.6 %shard_map.239.result = f32[8,128]{1,0:T(8,128)S(1)} custom-call(f32[128,128]{1,0:T(8,128)S(1)} %bitcast.5, s32[1,256]{1,0:T(1,128)S(1)} %bitcast.8, s32[1,256]{1,0:T(1,128)S(1)} %bitcast.9, s32[256,128]{1,0:T(8,128)S(1)} %bitcast.6, bf16[512,512]{1,0:T(8,128)(2,1)S(1)} %copy-done.5, bf16[512,512]{1,0:T(8,128)(2,1)S(1)} %copy-done.4, ...), custom_call_target="tpu_custom_call" | custom-call | tf_op jit(solution)/shard_map/pallas_call | solution.py:586
  56.3 0.6 copy-done.11
  56.9 20.1 %shard_map.240 = (f32[6,2]{1,0:T(8,128)}, f32[3,4]{1,0:T(4,128)}, f32[3,4]{1,0:T(4,128)}) custom-call(f32[8,128]{1,0:T(8,128)} %copy-done.11, f32[128,128]{1,0:T(8,128)} %bitcast.4, s32[1,256]{1,0:T(1,128)} %bitcast.7, s32[2]{0:T(128)} %listed.3, f32[4,8,128]{2,1,0:T(8,128)} %get-tuple-element.6.near, f32[128,256]{1,0:T(8,128)} %constant.42.clone.sv, ...), custom_call_target="tpu_custom_call" | custom-call | tf_op jit(solution)/shard_map/pallas_call | solution.py:594
  77.0 1.3 %copy.28 = f32[6,2]{0,1:T(2,128)} copy(f32[6,2]{1,0:T(8,128)} %get-tuple-element.7) | data formatting | bytes 96 | tf_op jit(solution)/shard_map/pallas_call | solution.py:594
  78.3 1.3 %copy.31 = f32[3,4]{1,0:T(4,128)} copy(f32[3,4]{1,0:T(4,128)} %get-tuple-element.14) | data formatting | bytes 96
  79.6 1.3 %copy.32 = f32[3,4]{1,0:T(4,128)} copy(f32[3,4]{1,0:T(4,128)} %get-tuple-element.15) | data formatting | bytes 96
  (4 shorter events, 0.0 us)
Async XLA Ops:
  23.0 1.2 %copy-start = (bf16[8,256,256]{2,1,0:T(8,128)(2,1)S(1)}, bf16[8,256,256]{2,1,0:T(8,128)(2,1)}, u32[]{:S(2)}) copy-start(bf16[8,256,256]{2,1,0:T(8,128)(2,1)} %constant.37.clone.refs_9_) | copy-start | bytes 3145732
  24.3 1.2 %copy-start.1 = (bf16[8,256,256]{2,1,0:T(8,128)(2,1)S(1)}, bf16[8,256,256]{2,1,0:T(8,128)(2,1)}, u32[]{:S(2)}) copy-start(bf16[8,256,256]{2,1,0:T(8,128)(2,1)} %constant.36.clone.refs_8_) | copy-start | bytes 3145732
  25.5 1.0 %copy-start.2 = (bf16[512,512]{1,0:T(8,128)(2,1)S(1)}, bf16[512,512]{1,0:T(8,128)(2,1)}, u32[]{:S(2)}) copy-start(bf16[512,512]{1,0:T(8,128)(2,1)} %constant.35.clone.refs_7_) | copy-start | bytes 1572868
  26.5 1.0 %copy-start.3 = (bf16[512,512]{1,0:T(8,128)(2,1)S(1)}, bf16[512,512]{1,0:T(8,128)(2,1)}, u32[]{:S(2)}) copy-start(bf16[512,512]{1,0:T(8,128)(2,1)} %constant.34.clone.refs_6_) | copy-start | bytes 1572868
  27.6 1.0 %copy-start.4 = (bf16[512,512]{1,0:T(8,128)(2,1)S(1)}, bf16[512,512]{1,0:T(8,128)(2,1)}, u32[]{:S(2)}) copy-start(bf16[512,512]{1,0:T(8,128)(2,1)} %constant.33.clone.refs_5_) | copy-start | bytes 1572868
  28.6 1.0 %copy-start.5 = (bf16[512,512]{1,0:T(8,128)(2,1)S(1)}, bf16[512,512]{1,0:T(8,128)(2,1)}, u32[]{:S(2)}) copy-start(bf16[512,512]{1,0:T(8,128)(2,1)} %constant.32.clone.refs_4_) | copy-start | bytes 1572868
  29.7 1.0 %copy-start.6 = (f32[128,768]{1,0:T(8,128)S(1)}, f32[128,768]{1,0:T(8,128)}, u32[]{:S(2)}) copy-start(f32[128,768]{1,0:T(8,128)} %constant.41.clone.refs_14_) | copy-start | bytes 1179652
  30.7 0.8 %copy-start.7 = (f32[8,16,128]{2,1,0:T(8,128)S(1)}, f32[8,16,128]{2,1,0:T(8,128)}, u32[]{:S(2)}) copy-start(f32[8,16,128]{2,1,0:T(8,128)} %get-tuple-element.5) | copy-start | bytes 196612
  31.5 0.9 %copy-start.8 = (f32[512,128]{1,0:T(8,128)S(1)}, f32[512,128]{1,0:T(8,128)}, u32[]{:S(2)}) copy-start(f32[512,128]{1,0:T(8,128)} %constant.31.clone.refs_15_) | copy-start | bytes 786436
  32.4 0.9 %copy-start.9 = (s32[1,32768]{1,0:T(1,128)S(1)}, s32[1,32768]{1,0:T(1,128)}, u32[]{:S(2)}) copy-start(s32[1,32768]{1,0:T(1,128)} %param.30) | copy-start | bytes 393220
  33.3 0.9 %copy-start.10 = (f32[128,256]{1,0:T(8,128)S(1)}, f32[128,256]{1,0:T(8,128)}, u32[]{:S(2)}) copy-start(f32[128,256]{1,0:T(8,128)} %constant.40.clone.refs_13_) | copy-start | bytes 393220
  34.3 0.7 copy-start.12
  34.9 0.7 copy-start.13
  56.3 0.6 copy-start.11

commit v2 on v1

--- a/solution.py
+++ b/solution.py
@@ -1,5 +1,3 @@
-import functools
-
 import jax
 import jax.numpy as jnp
 import ml_dtypes
@@ -8,8 +6,6 @@
 from jax.experimental import pallas as pl
 from jax.experimental.pallas import tpu as pltpu
 from jax.sharding import PartitionSpec as P
-
-MERGED = False
 
 EXACT = lax.Precision.HIGHEST
 F32 = jnp.float32
@@ -133,109 +129,112 @@
     return out + jnp.dot(a_high, b_low, preferred_element_type=F32)
 
 
-def plane_peer(other):
+FAR = (4, 5, 3, 6, 2, 7, 1, 0)
+
+
+def each_peer(action):
     dev = lax.axis_index("dev")
-    return (dev // 16) * 16 + (dev + other) % 16
-
-
-def column_peer(other):
-    return (lax.axis_index("dev") + 16 * other) % 128
-
-
-def greet(both_cores):
+    for across in FAR:
+        level = (dev // 16 + across) % 8
+
+        def one(j, carry, level=level):
+            action(level * 16 + (dev + j) % 16)
+            return carry
+
+        lax.fori_loop(1 if across == 0 else 0, 16, one, 0)
+
+
+def sibling():
+    return ((lax.axis_index("grp") + 1) % 2, lax.axis_index("dev"))
+
+
+def greet():
     barrier = pltpu.get_barrier_semaphore()
     grp = lax.axis_index("grp")
-    peers = [(grp, plane_peer(j)) for j in range(1, 16)]
-    peers += [(grp, column_peer(j)) for j in range(1, 8)]
-    if both_cores:
-        peers += [((grp + 1) % 2, plane_peer(j)) for j in range(16)]
-    for peer in peers:
+
+    def signal(peer):
         pl.semaphore_signal(barrier, inc=1, device_id=peer, device_id_type=MESH)
-    pl.semaphore_wait(barrier, len(peers))
-
-
-def copy_to(src, dst, send, recv, peer):
-    return pltpu.make_async_remote_copy(
-        src_ref=src, dst_ref=dst, send_sem=send, recv_sem=recv,
-        device_id=peer, device_id_type=MESH,
-    )
-
-
-def gather_start(rows, row, cores, sems):
+
+    each_peer(lambda dev: signal((grp, dev)))
+    signal(sibling())
+    return barrier
+
+
+def gather_start(note, rows, send, recv):
     dev, grp = lax.axis_index("dev"), lax.axis_index("grp")
-    level = dev // 16
-    mine = dev % 16 + (16 * grp if cores == 2 else 0)
-    rows[level, pl.ds(mine, 1), :] = row
-    copies = []
-    for core in range(cores):
-        for j in range(1 - core, 16):
-            peer = ((grp + core) % 2, plane_peer(j))
-            n = 16 * core + j
-            here = rows.at[level, pl.ds(mine, 1)]
-            copies.append(copy_to(here, here, sems[0].at[n], sems[1].at[n], peer))
-    for copy in copies:
-        copy.start()
-    return copies
-
-
-def gather_across(rows, sems):
-    level, grp = lax.axis_index("dev") // 16, lax.axis_index("grp")
-    here = rows.at[level]
-    copies = [
-        copy_to(here, here, sems[2].at[j], sems[3].at[j], (grp, column_peer(j)))
-        for j in range(1, 8)
-    ]
-    for copy in copies:
-        copy.start()
-    return copies
-
-
-def wait_all(copies):
-    for copy in copies:
-        copy.wait()
-
-
-def widened(b_ref, conn_ref, d):
-    del conn_ref
-    parts = [b_ref[i, pl.ds(d, 8, stride=3), :] for i in range(6)]
-    parts.append(jnp.zeros((8, 116), F32))
-    return jnp.concatenate(parts, axis=1)
-
-
-def partition_row(disp, probe, b_ref, conn_ref, listed, near_ref):
+    src, dst = note.at[pl.ds(0, 1)], rows.at[pl.ds(dev, 1)]
+
+    def start(peer):
+        pltpu.make_async_remote_copy(
+            src_ref=src, dst_ref=dst, send_sem=send, recv_sem=recv,
+            device_id=(grp, peer), device_id_type=MESH,
+        ).start()
+
+    each_peer(start)
+    pltpu.make_async_copy(src, dst, recv).start()
+
+
+def gather_wait(rows, send, recv):
+    pltpu.make_async_copy(rows, rows, recv).wait()
+    most = rows.at[pl.ds(0, 127)]
+    pltpu.make_async_copy(most, most, send).wait()
+
+
+def partition_row(disp, probe, b_ref, conn_ref, listed, flat, near_ref):
     lane, sub = iota((8, 128), 1), iota((8, 128), 0)
-    conn = conn_ref[...]
-    conn = jnp.concatenate([conn] * 6 + [jnp.full((8, 116), -1, jnp.int32)], axis=1)
-    weights = [widened(b_ref, conn_ref, d) for d in range(3)]
-    total = jnp.zeros((8, 128), F32)
-    for uv, field in enumerate((disp, probe)):
-        base = jnp.zeros((8, 128), F32)
-        for d in range(3):
+    flat[...] = jnp.zeros((128, 128), F32)
+    for i in range(6):
+        flat[pl.ds(2 * i, 2), pl.ds(0, 24)] = b_ref[i]
+    axis = lane % 3
+    spread = (lane // 3 == sub).astype(F32)
+    conn = jnp.dot(conn_ref[...].astype(F32), spread, preferred_element_type=F32)
+    values = []
+    for field in (disp, probe):
+        values.append(
+            [
+                jnp.where(axis == 0, field[0, n], jnp.where(axis == 1, field[1, n], field[2, n]))
+                for n in range(4)
+            ]
+        )
+    blocks, nears = [], []
+    for p in range(2):
+        c = jnp.broadcast_to(conn[p : p + 1], (8, 128))
+        block = ((c == 4.0) & (axis == sub - 2)) | ((c == 5.0) & (axis == sub - 5))
+        block = block.astype(F32)
+        for uv in range(2):
             value = jnp.zeros((8, 128), F32)
             for n in range(4):
-                value = jnp.where(conn == n, field[d, n], value)
-            base = base + weights[d] * value
-        total = total + (pltpu.roll(base, 16, 1) if uv else base)
-    for end in range(2):
-        for d in range(3):
-            one = jnp.where(conn == 4 + end, weights[d], 0.0)
-            total = total + pltpu.roll(one, 32 + 48 * end + 16 * d, 1)
+                value = jnp.where(c == float(n), values[uv][n], value)
+            block = jnp.where(sub == uv, value, block)
+        blocks.append(block)
+        nears.append([((c == float(n)) & (axis == sub)).astype(F32) for n in range(4)])
+    heap = blocks + [nears[p][n] for n in range(4) for p in range(2)]
+    w = lax.dot_general(
+        jnp.concatenate(heap, axis=0), flat[...], (((1,), (1,)), ((), ())),
+        precision=EXACT, preferred_element_type=F32,
+    )
+    even = lane % 2 == 0
+    x = jnp.where(even, w[:8], w[8:16])
+    total = jnp.where(sub == 0, x, 0.0)
+    for g in range(1, 8):
+        total = total + pltpu.roll(jnp.where(sub == g, x, 0.0), 16 * g, 1)
     row = jnp.sum(total, axis=0, keepdims=True)
-    for d in range(3):
-        for uv, field in enumerate((disp, probe)):
-            for way in range(2):
-                value = jnp.zeros((1, 128), F32)
-                for n in range(4):
-                    value = jnp.where(
-                        jnp.full((1, 128), listed[1 - way], jnp.int32) == n, field[d, n], value
-                    )
-                row = jnp.where(lane[:1] == 16 * d + 12 + 2 * way + uv, value, row)
     for n in range(4):
-        near = jnp.zeros((8, 128), F32)
-        for d in range(3):
-            one = jnp.sum(jnp.where(conn == n, weights[d], 0.0), axis=0, keepdims=True)
-            near = jnp.where(sub == d, one, near)
-        near_ref[n] = near
+        at = 16 + 16 * n
+        near_ref[n] = jnp.where(even, w[at : at + 8], w[at + 8 : at + 16])
+    for way in range(2):
+        want = jnp.full((1, 128), listed[1 - way], jnp.int32)
+        for uv in range(2):
+            sent = jnp.zeros((1, 128), F32)
+            for n in range(4):
+                field = (disp, probe)[uv]
+                third = lane[:1] // 16
+                value = jnp.where(
+                    third == 0, field[0, n], jnp.where(third == 1, field[1, n], field[2, n])
+                )
+                sent = jnp.where(want == n, value, sent)
+            place = (lane[:1] < 48) & (lane[:1] % 16 == 12 + 2 * way + uv)
+            row = jnp.where(place, sent, row)
     return row
 
 
@@ -446,58 +445,70 @@
     return exact_dot(lanes, c.summary[...])
 
 
-def finish(rows, results, owner, listed, near, c, stress_ref, force_ref, image_ref):
-    dev = lax.axis_index("dev")
+def finish(c, listed, out_ref):
+    dev, grp = lax.axis_index("dev"), lax.axis_index("grp")
     sub, lane = iota((8, 128), 0), iota((8, 128), 1)
     step = jnp.where(sub < 2, 0, jnp.where(sub < 4, -1, 1))
     point = (2 * (jnp.full((8, 128), dev, jnp.int32) + step) + sub % 2).astype(F32)
     point = jnp.where(sub < 6, point, NONE)
-    found, masked = point_rows(rows, point, 1, c.spread_v[...])
-    direction = exact_dot(masked, c.expand[...])
+    found, masked = point_rows(c.rows[...], point, 1, c.small[:, 1024:1280])
+    direction = exact_dot(masked, c.small[:, 1280:1408])
     index = iota((8, 256), 1).astype(F32)
     wide = jnp.concatenate([point, point], axis=1)
-    owners = jnp.broadcast_to(owner.astype(F32), (8, 256))
+    owners = jnp.broadcast_to(c.owner[...].astype(F32), (8, 256))
     who = jnp.sum(jnp.where(index == wide, owners, 0.0), axis=1, keepdims=True)
     rank = jnp.sum(
         jnp.where((owners == who) & (index < wide), 1.0, 0.0), axis=1, keepdims=True
     )
     slot = jnp.floor(rank * 0.5)
-    level = jnp.floor(who * 0.0625)
-    place = who + 16.0 * level + 16.0 * (rank - 2.0 * slot)
-    value = exact_dot((index == place).astype(F32), results)
+    core = jnp.full((8, 1), grp, jnp.int32).astype(F32)
+    ours = (rank - 2.0 * slot) == core
+    pick = ((lanes_f32() == who) & ours).astype(F32)
+
+    gather_wait(c.results, c.send_b, c.recv_b)
+    value = exact_dot(pick, c.results[...])
     value = jnp.where(slot > 0.5, pltpu.roll(value, 64, 1), value)
     value = jnp.where(lane < 64, value, 0.0)
+    c.swap[0] = value
+    copy = pltpu.make_async_remote_copy(
+        src_ref=c.swap.at[0], dst_ref=c.swap.at[1], send_sem=c.send_c, recv_sem=c.recv_c,
+        device_id=sibling(), device_id_type=MESH,
+    )
+    copy.start()
+    copy.wait()
+    value = value + c.swap[1]
+    out_ref[0] = value
     terms = value * jnp.where(lane < 6, 1.0, direction)
-    dealt = exact_dot(terms, c.deal[...])
+    dealt = exact_dot(terms, c.small[:, 1408:1664])
     own_lane = lane % 2 == sub % 2
-    out_sub, out_lane = sub, lane
-    column = jnp.where(out_lane == 0, value[0:1], 0.0)
-    del column
-    picks = [
-        jnp.sum(jnp.where(out_lane == out_sub, value[p : p + 1], 0.0), axis=1, keepdims=True)
-        for p in range(2)
-    ]
-    stress_ref[...] = jnp.where(out_lane == 0, picks[0], picks[1])[:6, :2]
-    for half, ref in enumerate((force_ref, image_ref)):
+    twelve = lane % 16 < 12
+    for half in range(2):
         y = jnp.where(own_lane, dealt[:, 128 * half : 128 * half + 128], 0.0)
         mine = jnp.sum(jnp.where(sub < 2, y, 0.0), axis=0, keepdims=True)
         linked = y * found
         before = jnp.sum(jnp.where((sub == 2) | (sub == 3), linked, 0.0), axis=0, keepdims=True)
         after = jnp.sum(jnp.where((sub == 4) | (sub == 5), linked, 0.0), axis=0, keepdims=True)
-        twelve = lane % 16 < 12
         out = jnp.zeros((8, 128), F32)
         for n in range(4):
-            got = jnp.sum(near[n] * mine, axis=1, keepdims=True)
+            got = jnp.sum(c.near[n] * jnp.where(lane < 12, mine, 0.0), axis=1, keepdims=True)
             out = jnp.where(lane == n, got, out)
         for end, row, lead in ((0, before, 5), (1, after, 2)):
             part = jnp.where(twelve & (lane // 16 == sub + lead) & (sub < 3), row, 0.0)
             got = jnp.sum(part, axis=1, keepdims=True)
             out = out + jnp.where(lane == listed[end], got, 0.0)
-        ref[...] = out[:3, :4]
-
-
-TABLES = ("lf_h", "lf_l", "li_h", "li_l", "rf_h", "rf_l", "ri_h", "ri_l", "green")
-SMALL = ("spread_u", "splat", "summary", "spread_v", "expand", "deal")
+        out_ref[1 + half] = out
+
+
+TABLES = {
+    "lf": ((2, 512, 512), BF16),
+    "rf": ((2, 8, 256, 256), BF16),
+    "li": ((2, 512, 512), BF16),
+    "ri": ((2, 8, 256, 256), BF16),
+    "green": ((9, 256, 128), F32),
+    "small": ((128, 1664), F32),
+    "summary": ((512, 128), F32),
+    "phase": ((256, 128), jnp.int32),
+}
 WORK = {
     "chi": ((256, 256), F32),
     "spec": ((192, 256), F32),
@@ -506,7 +517,15 @@
     "u": ((512, 768), F32),
     "f": ((512, 768), F32),
     "sums": ((512, 128), F32),
+    "flat": ((128, 128), F32),
+    "near": ((4, 8, 128), F32),
+    "note": ((8, 128), F32),
+    "rows": ((128, 128), F32),
+    "results": ((128, 128), F32),
+    "swap": ((2, 8, 128), F32),
 }
+SEMS = ("send", "recv", "send_b", "recv_b", "send_c", "recv_c")
+INPUTS = ("disp", "probe", "b", "conn", "listed", "owner", "counts")
 
 
 class Bag:
@@ -515,91 +534,86 @@
 
 
 def constants():
-    lf, rf, li, ri = dft_tables()
-    out = {"green": green_tables(), "summary": summary_table()}
-    for name, table in (("lf", lf), ("li", li), ("rf", rf), ("ri", ri)):
-        out[name + "_h"], out[name + "_l"] = two_parts(table)
-    names = ("spread_u", "splat", "spread_v", "expand", "deal")
-    out.update(zip(names, message_tables()))
+    out = dict(zip(("lf", "rf", "li", "ri"), (np.stack(two_parts(t)) for t in dft_tables())))
+    spread_u, splat, spread_v, expand, deal = message_tables()
+    out["small"] = np.concatenate([spread_u, splat, spread_v, expand, deal], axis=1)
+    out["green"], out["summary"] = green_tables(), summary_table()
     return out
 
 
-def splats(rows, owner, counts, c):
-    point, turns = my_points(owner, counts)
-    _, masked = point_rows(rows, point, 0, c.spread_u[...])
-    strain = exact_dot(masked, c.splat[...])
-    e = [
+def splats(c, point):
+    _, masked = point_rows(c.rows[...], point, 0, c.small[:, :256])
+    strain = exact_dot(masked, c.small[:, 256:1024])
+    return [
         [jnp.broadcast_to(strain[q : q + 1, 128 * i : 128 * i + 128], (8, 128)) for i in range(6)]
         for q in range(2)
     ]
-    return e, turns
+
+
+def main_kernel(*refs):
+    names = INPUTS + tuple(k + "_in" for k in TABLES) + ("out",) + tuple(TABLES) + tuple(WORK)
+    c = Bag(**dict(zip(names + SEMS + ("loads",), refs)))
+    loads = {
+        k: pltpu.make_async_copy(getattr(c, k + "_in"), getattr(c, k), c.loads.at[n])
+        for n, k in enumerate(TABLES)
+    }
+    for k in ("phase", "lf", "rf", "small", "li", "ri", "green", "summary"):
+        loads[k].start()
+    barrier = greet()
+    row = partition_row(c.disp, c.probe, c.b, c.conn, c.listed, c.flat, c.near)
+    c.note[...] = jnp.broadcast_to(row, (8, 128))
+    pl.semaphore_wait(barrier, 128)
+    gather_start(c.note, c.rows, c.send, c.recv)
+    for k in TABLES:
+        loads[k].wait()
+    c.lf_h, c.lf_l, c.li_h, c.li_l = c.lf.at[0], c.lf.at[1], c.li.at[0], c.li.at[1]
+    c.rf_h, c.rf_l, c.ri_h, c.ri_l = c.rf.at[0], c.rf.at[1], c.ri.at[0], c.ri.at[1]
+    phase_spectrum(c)
+    point, turns = my_points(c.owner[...], c.counts[...])
+    gather_wait(c.rows, c.send, c.recv)
+    c.note[...] = solve(c, splats(c, point), turns)
+    gather_start(c.note, c.results, c.send_b, c.recv_b)
+    finish(c, c.listed, c.out)
+
+
+def last_kernel(packed, stress, force, image):
+    stress[...] = packed[0, :2, :6]
+    force[...] = packed[1, :3, :4]
+    image[...] = packed[2, :3, :4]
 
 
 VM = pl.BlockSpec(memory_space=pltpu.VMEM)
 SM = pl.BlockSpec(memory_space=pltpu.SMEM)
-SEMS = [
-    pltpu.SemaphoreType.DMA((32,)), pltpu.SemaphoreType.DMA((32,)),
-    pltpu.SemaphoreType.DMA((8,)), pltpu.SemaphoreType.DMA((8,)),
-]
-
-
-def first_kernel(disp, probe, b, conn, listed, rows_out, near_out, rows, *sems):
-    row = partition_row(disp, probe, b, conn, listed, near_out)
-    greet(False)
-    wait_all(gather_start(rows, row, 1, sems))
-    wait_all(gather_across(rows, sems))
-    rows_out[...] = rows[...]
-
-
-def second_kernel(names, *refs):
-    c = Bag(**dict(zip(names, refs)))
-    phase_spectrum(c)
-    e, turns = splats(c.rows[...], c.owner[...], c.counts[...], c)
-    c.out[...] = solve(c, e, turns)
-
-
-def third_kernel(result, gathered, owner, listed, near, sv, ex, de, s_out, f_out, i_out, rows, *sems):
-    c = Bag(spread_v=sv, expand=ex, deal=de)
-    greet(True)
-    wait_all(gather_start(rows, result[0:1, :], 2, sems))
-    wait_all(gather_across(rows, sems))
-    results = rows[...].reshape(256, 128)
-    finish(gathered[...], results, owner[...], listed, near, c, s_out, f_out, i_out)
+FAR_OFF = pl.BlockSpec(memory_space=pltpu.HBM)
 
 
 def on_device(disp, probe, strain_disp, conn, halo_rows, owner, counts, phase):
     table = {k: jnp.asarray(v) for k, v in constants().items()}
-    owner, counts = owner.reshape(1, 256), counts.reshape(1, 256)
-    phase = phase.reshape(256, 128)
+    table["phase"] = phase.reshape(256, 128)
     shape = jax.ShapeDtypeStruct
-    rows, near = pl.pallas_call(
-        first_kernel,
-        out_shape=(shape((8, 16, 128), F32), shape((4, 8, 128), F32)),
-        in_specs=[SM, SM, VM, VM, SM],
-        out_specs=(VM, VM),
-        scratch_shapes=[pltpu.VMEM((8, 16, 128), F32)] + SEMS,
-        compiler_params=pltpu.CompilerParams(collective_id=0, has_side_effects=True),
-    )(disp, probe, strain_disp, conn, halo_rows)
-    rows = rows.reshape(128, 128)
-    names = ("rows", "owner", "counts", "phase") + TABLES + SMALL[:3]
-    args = [rows, owner, counts, phase] + [table[n] for n in TABLES + SMALL[:3]]
-    result = pl.pallas_call(
-        functools.partial(second_kernel, names + ("out",) + tuple(WORK)),
-        out_shape=shape((8, 128), F32),
-        in_specs=[VM] * len(args),
+    packed = pl.pallas_call(
+        main_kernel,
+        out_shape=shape((3, 8, 128), F32),
+        in_specs=[SM, SM, VM, VM, SM, VM, VM] + [FAR_OFF] * len(TABLES),
         out_specs=VM,
-        scratch_shapes=[pltpu.VMEM(*v) for v in WORK.values()],
-        compiler_params=pltpu.CompilerParams(vmem_limit_bytes=48 << 20),
-    )(*args)
-    outs = pl.pallas_call(
-        third_kernel,
-        out_shape=(shape((6, 2), F32), shape((3, 4), F32), shape((3, 4), F32)),
-        in_specs=[VM, VM, VM, SM, VM, VM, VM, VM],
+        scratch_shapes=[pltpu.VMEM(*v) for v in TABLES.values()]
+        + [pltpu.VMEM(*v) for v in WORK.values()]
+        + [pltpu.SemaphoreType.DMA] * len(SEMS)
+        + [pltpu.SemaphoreType.DMA((8,))],
+        compiler_params=pltpu.CompilerParams(
+            collective_id=0, has_side_effects=True, vmem_limit_bytes=48 << 20
+        ),
+    )(
+        disp, probe, strain_disp.transpose(0, 2, 1), conn.T, halo_rows,
+        owner.reshape(1, 256), counts.reshape(1, 256), *[table[k] for k in TABLES],
+    )
+    stress, force, image = pl.pallas_call(
+        last_kernel,
+        out_shape=(shape((2, 6), F32), shape((3, 4), F32), shape((3, 4), F32)),
+        in_specs=[VM],
         out_specs=(VM, VM, VM),
-        scratch_shapes=[pltpu.VMEM((8, 32, 128), F32)] + SEMS,
-        compiler_params=pltpu.CompilerParams(collective_id=1, has_side_effects=True),
-    )(result, rows, owner, halo_rows, near, *[table[n] for n in SMALL[3:]])
-    return outs
+    )(packed)
+    return stress.T, force, image
 
 
 def solution(mesh):

time: 81.6 us -> 63.6 us (0.78)
  Pallas kernels: 60.4 us -> 50.4 us
  local copies, waits for them, and re-layouts: 19.8 us -> 12.1 us
    pallas_call x3 -> x2, Pallas kernels: 60.4 us -> 50.4 us  [the longest x1 49.1 us: on_device(): pl.pallas_call(main_kernel, out_shape=shape((3, 8, 128), F32), in_specs=[...]
    unnamed x32 -> x28, local copies, waits for them, and re-layouts: 18.4 us -> 12.1 us
    pallas_call x1 -> x0, local copies, waits for them, and re-layouts: 1.33 us -> none  [on_device(): pl.pallas_call(third_kernel, out_shape=(shape((6, 2), F32), shape((3, 4),...]
where the time goes in v2:
time: 63.6 us; the launch traced here: 63.1 us
  Pallas kernels  50.4 us (79%)
  local copies, waits for them, and re-layouts  12.1 us (19%)
  between operations  0.67 us (1%)
    pallas_call x1, Pallas kernels, on_device(): pl.pallas_call(main_kernel, out_shape=shape((3, 8, 128), F32), in_specs=[...  49.1 us
    unnamed x28, local copies, waits for them, and re-layouts  12.1 us
    pallas_call x1, Pallas kernels, on_device(): pl.pallas_call(last_kernel, out_shape=(shape((2, 6), F32), shape((3, 4),...  1.29 us

profile of v2, /device:TPU:1, one launch (start us, length us, event | category | flops | bytes accessed | tf_op | source)
XLA Modules:
  0.0 63.1 jit_solution(2140180771769747493)
XLA Ops:
  0.6 0.0 copy-start
  0.6 1.3 %copy-done = f32[9,256,128]{2,1,0:T(8,128)S(1)} copy-done((f32[9,256,128]{2,1,0:T(8,128)S(1)}, f32[9,256,128]{2,1,0:T(8,128)}, u32[]{:S(2)}) %copy-start) | copy-done | bytes 1179672
  1.9 0.0 copy-start.1
  1.9 1.2 %copy-done.1 = bf16[2,512,512]{2,1,0:T(8,128)(2,1)S(1)} copy-done((bf16[2,512,512]{2,1,0:T(8,128)(2,1)S(1)}, bf16[2,512,512]{2,1,0:T(8,128)(2,1)}, u32[]{:S(2)}) %copy-start.1) | copy-done | bytes 1048600
  3.1 0.0 copy-start.2
  3.1 1.2 %copy-done.2 = bf16[2,512,512]{2,1,0:T(8,128)(2,1)S(1)} copy-done((bf16[2,512,512]{2,1,0:T(8,128)(2,1)S(1)}, bf16[2,512,512]{2,1,0:T(8,128)(2,1)}, u32[]{:S(2)}) %copy-start.2) | copy-done | bytes 1048600
  4.4 0.0 copy-start.3
  4.4 1.2 %copy-done.3 = f32[128,1664]{1,0:T(8,128)S(1)} copy-done((f32[128,1664]{1,0:T(8,128)S(1)}, f32[128,1664]{1,0:T(8,128)}, u32[]{:S(2)}) %copy-start.3) | copy-done | bytes 851992
  5.5 0.0 copy-start.4
  5.5 0.9 %copy-done.4 = f32[512,128]{1,0:T(8,128)S(1)} copy-done((f32[512,128]{1,0:T(8,128)S(1)}, f32[512,128]{1,0:T(8,128)}, u32[]{:S(2)}) %copy-start.4) | copy-done | bytes 262168
  6.5 0.0 copy-start.5
  6.5 0.9 %copy-done.5 = s32[1,32768]{1,0:T(1,128)S(1)} copy-done((s32[1,32768]{1,0:T(1,128)S(1)}, s32[1,32768]{1,0:T(1,128)}, u32[]{:S(2)}) %copy-start.5) | copy-done | bytes 131096
  7.4 0.0 copy-start.7
  7.4 0.7 %copy-done.7 = f32[6,24,2]{1,2,0:T(2,128)S(1)} copy-done((f32[6,24,2]{1,2,0:T(2,128)S(1)}, f32[6,24,2]{1,2,0:T(2,128)}, u32[]{:S(2)}) %copy-start.7) | copy-done | bytes 1176
  8.1 0.0 copy-start.8
  8.1 0.7 %copy-done.8 = f32[3,4]{1,0:T(4,128)S(1)} copy-done((f32[3,4]{1,0:T(4,128)S(1)}, f32[3,4]{1,0:T(4,128)}, u32[]{:S(2)}) %copy-start.8) | copy-done | bytes 72
  8.7 0.0 copy-start.9
  8.7 0.7 %copy-done.9 = f32[3,4]{1,0:T(4,128)S(1)} copy-done((f32[3,4]{1,0:T(4,128)S(1)}, f32[3,4]{1,0:T(4,128)}, u32[]{:S(2)}) %copy-start.9) | copy-done | bytes 72
  9.4 0.0 copy-start.10
  9.4 0.7 %copy-done.10 = s32[8,2]{0,1:T(2,128)S(1)} copy-done((s32[8,2]{0,1:T(2,128)S(1)}, s32[8,2]{0,1:T(2,128)}, u32[]{:S(2)}) %copy-start.10) | copy-done | bytes 88
  10.1 0.0 copy-start.11
  10.1 0.7 %copy-done.11 = s32[256,1]{0,1:T(1,128)S(1)} copy-done((s32[256,1]{0,1:T(1,128)S(1)}, s32[256,1]{0,1:T(1,128)}, u32[]{:S(2)}) %copy-start.11) | copy-done | bytes 1048
  10.8 0.0 copy-start.12
  10.8 0.7 %copy-done.12 = s32[256]{0:T(256)S(1)} copy-done((s32[256]{0:T(256)S(1)}, s32[256]{0:T(256)}, u32[]{:S(2)}) %copy-start.12) | copy-done | bytes 1048
  11.5 0.0 copy-start.13
  11.5 0.7 %copy-done.13 = s32[2]{0:T(128)S(1)} copy-done((s32[2]{0:T(128)S(1)}, s32[2]{0:T(128)}, u32[]{:S(2)}) %copy-start.13) | copy-done | bytes 32
  12.1 49.1 %shard_map.166.packed = f32[3,8,128]{2,1,0:T(8,128)S(1)} custom-call(f32[3,4]{1,0:T(4,128)S(1)} %copy-done.8, f32[3,4]{1,0:T(4,128)S(1)} %copy-done.9, f32[6,2,24]{2,1,0:T(2,128)S(1)} %bitcast.7, s32[2,8]{1,0:T(2,128)S(1)} %bitcast.8, s32[2]{0:T(128)S(1)} %copy-done.13, s32[1,256]{1,0:T(1,128)S(1)} %bitcast.9, s32[1,256]{1,0:T(1,128)S(1)} %bitcast.10, ...), custom_call_target="tpu_custom_call" | custom-call | tf_op jit(solution)/shard_map/pallas_call | solution.py:594
  61.2 0.0 copy-start.6
  61.2 0.6 copy-done.6
  61.8 1.3 %shard_map.167 = (f32[2,6]{1,0:T(2,128)}, f32[3,4]{1,0:T(4,128)}, f32[3,4]{1,0:T(4,128)}) custom-call(f32[3,8,128]{2,1,0:T(8,128)} %copy-done.6), custom_call_target="tpu_custom_call" | custom-call | tf_op jit(solution)/shard_map/pallas_call | solution.py:610
Async XLA Ops:
  0.6 1.3 %copy-start = (f32[9,256,128]{2,1,0:T(8,128)S(1)}, f32[9,256,128]{2,1,0:T(8,128)}, u32[]{:S(2)}) copy-start(f32[9,256,128]{2,1,0:T(8,128)} %constant.19.clone.refs_11_) | copy-start | bytes 3538948
  1.9 1.2 %copy-start.1 = (bf16[2,512,512]{2,1,0:T(8,128)(2,1)S(1)}, bf16[2,512,512]{2,1,0:T(8,128)(2,1)}, u32[]{:S(2)}) copy-start(bf16[2,512,512]{2,1,0:T(8,128)(2,1)} %constant.16.clone.refs_9_) | copy-start | bytes 3145732
  3.1 1.2 %copy-start.2 = (bf16[2,512,512]{2,1,0:T(8,128)(2,1)S(1)}, bf16[2,512,512]{2,1,0:T(8,128)(2,1)}, u32[]{:S(2)}) copy-start(bf16[2,512,512]{2,1,0:T(8,128)(2,1)} %constant.14.clone.refs_7_) | copy-start | bytes 3145732
  4.4 1.2 %copy-start.3 = (f32[128,1664]{1,0:T(8,128)S(1)}, f32[128,1664]{1,0:T(8,128)}, u32[]{:S(2)}) copy-start(f32[128,1664]{1,0:T(8,128)} %constant.18.clone.refs_12_) | copy-start | bytes 2555908
  5.5 0.9 %copy-start.4 = (f32[512,128]{1,0:T(8,128)S(1)}, f32[512,128]{1,0:T(8,128)}, u32[]{:S(2)}) copy-start(f32[512,128]{1,0:T(8,128)} %constant.20.clone.refs_13_) | copy-start | bytes 786436
  6.5 0.9 %copy-start.5 = (s32[1,32768]{1,0:T(1,128)S(1)}, s32[1,32768]{1,0:T(1,128)}, u32[]{:S(2)}) copy-start(s32[1,32768]{1,0:T(1,128)} %param.22) | copy-start | bytes 393220
  7.4 0.7 %copy-start.7 = (f32[6,24,2]{1,2,0:T(2,128)S(1)}, f32[6,24,2]{1,2,0:T(2,128)}, u32[]{:S(2)}) copy-start(f32[6,24,2]{1,2,0:T(2,128)} %param.17) | copy-start | bytes 3460
  8.1 0.7 %copy-start.8 = (f32[3,4]{1,0:T(4,128)S(1)}, f32[3,4]{1,0:T(4,128)}, u32[]{:S(2)}) copy-start(f32[3,4]{1,0:T(4,128)} %refs_0_.1) | copy-start | bytes 148
  8.7 0.7 %copy-start.9 = (f32[3,4]{1,0:T(4,128)S(1)}, f32[3,4]{1,0:T(4,128)}, u32[]{:S(2)}) copy-start(f32[3,4]{1,0:T(4,128)} %refs_1_.1) | copy-start | bytes 148
  9.4 0.7 %copy-start.10 = (s32[8,2]{0,1:T(2,128)S(1)}, s32[8,2]{0,1:T(2,128)}, u32[]{:S(2)}) copy-start(s32[8,2]{0,1:T(2,128)} %param.18) | copy-start | bytes 196
  10.1 0.7 %copy-start.11 = (s32[256,1]{0,1:T(1,128)S(1)}, s32[256,1]{0,1:T(1,128)}, u32[]{:S(2)}) copy-start(s32[256,1]{0,1:T(1,128)} %param.20) | copy-start | bytes 3076
  10.8 0.7 %copy-start.12 = (s32[256]{0:T(256)S(1)}, s32[256]{0:T(256)}, u32[]{:S(2)}) copy-start(s32[256]{0:T(256)} %param.21) | copy-start | bytes 3076
  11.5 0.7 %copy-start.13 = (s32[2]{0:T(128)S(1)}, s32[2]{0:T(128)}, u32[]{:S(2)}) copy-start(s32[2]{0:T(128)} %refs_4_.1) | copy-start | bytes 28
  61.2 0.6 copy-start.6

commit v3 on v2

--- a/solution.py
+++ b/solution.py
@@ -31,24 +31,26 @@
 
 
 def dft_tables():
-    n32, n8, n4 = np.arange(32), np.arange(8), np.arange(4)
+    n32, n16, n8, n4 = np.arange(32), np.arange(16), np.arange(8), np.arange(4)
     f32 = np.exp(-2j * np.pi / 32 * np.outer(n32, n32))
     f8 = np.exp(-2j * np.pi / 8 * np.outer(n8, n8))
     f4 = np.exp(-2j * np.pi / 4 * np.outer(n4, n4))
-    left = np.einsum("ab,cd->cabd", f32, f8).reshape(256, 256)
-    left = np.block([[left.real, -left.imag], [left.imag, left.real]])
-    rights = []
+    lefts, rights = [], []
+    for odd in range(2):
+        half = np.exp(-2j * np.pi / 32 * np.outer(2 * n16 + odd, n16))
+        one = np.einsum("ab,cd->cabd", half, f8).reshape(128, 128)
+        lefts.append(np.block([[one.real, -one.imag], [one.imag, one.real]]))
     for k0 in range(8):
         turn = np.exp(-2j * np.pi / 32 * n4 * k0)[:, None] * f4
         one = np.einsum("ab,cd->acbd", turn, f32).reshape(128, 128)
         rights.append(np.block([[one.real, one.imag], [-one.imag, one.real]]))
-    right = np.stack(rights)
-    return left, right, left.T / VOXELS, right.transpose(0, 2, 1)
+    left, right = np.stack(lefts), np.stack(rights)
+    return left, right, left.transpose(0, 2, 1) / VOXELS, right.transpose(0, 2, 1)
 
 
 def green_tables():
     row, lane = np.arange(256)[:, None], np.arange(128)[None, :]
-    k = [row % 32 + 0 * lane, 8 * (lane // 32) + row // 32, lane % 32 + 0 * row]
+    k = [2 * (row % 16) + row % 32 // 16 + 0 * lane, 8 * (lane // 32) + row // 32, lane % 32 + 0 * row]
     freq = [np.where(v < 16, v, v - 32).astype(np.float64) for v in k]
     length = np.sqrt(np.maximum(sum(f * f for f in freq), 1.0))
     normal = [f / length for f in freq]
@@ -71,21 +73,18 @@
                 spread[uv, 1, 16 * d + 14 + uv, 80 + 16 * d + j] = 1.0
     splat = np.zeros((128, 6, 128), np.float32)
     expand = np.zeros((128, 128), np.float32)
+    weigh = np.zeros((128, 2, 128), np.float32)
     for g in range(8):
         for i in range(6):
             for p in range(2):
                 splat[16 * g + 2 * i + p, i, :] = 1.0
+                weigh[16 * g + 2 * i + p, p, i] = 1.0
                 for k in range(6):
                     expand[16 * g + 2 * i + p, 8 + 6 * i + k] = 1.0
-    deal = np.zeros((2, 128, 128), np.float32)
-    for i in range(6):
-        for p in range(2):
-            for lead in [0] + [32 + 16 * g for g in range(6)]:
-                deal[0, i, lead + 2 * i + p] = 1.0
-                for j in range(6):
-                    deal[1, 8 + 6 * j + i, lead + 2 * i + p] = 1.0
+                    weigh[16 * g + 2 * i + p, p, 8 + 6 * k + i] = 1.0
     pack = lambda a: a.transpose(1, 0, 2).reshape(128, -1)
-    return pack(spread[0]), splat.reshape(128, 768), pack(spread[1]), expand, pack(deal)
+    flat = lambda a: a.reshape(128, -1)
+    return pack(spread[0]), flat(splat), pack(spread[1]), expand, flat(weigh)
 
 
 def summary_table():
@@ -103,7 +102,7 @@
                 table[q, 7, :, lane] = 2.0 * project[i, j]
                 place = UPPER.index((min(i, j), max(i, j)))
                 table[q, 8 + place, :, lane] = -1.0
-    return (table.reshape(512, 128) / VOXELS).astype(np.float32)
+    return table.reshape(512, 128) / VOXELS
 
 
 def iota(shape, dim):
@@ -114,8 +113,10 @@
     return iota((8, 128), 1).astype(F32)
 
 
-def exact_dot(a, b):
-    return jnp.dot(a, b, precision=EXACT, preferred_element_type=F32)
+def two_dot(a, b):
+    high, low = split(a)
+    out = jnp.dot(jnp.concatenate([high, low], axis=0), b, preferred_element_type=F32)
+    return out[: a.shape[0]] + out[a.shape[0] :]
 
 
 def split(value):
@@ -243,9 +244,13 @@
     part = jnp.floor(point * 0.5)
     parity = point - 2.0 * part
     pick = jnp.concatenate([lane == part, lane == part - 1.0, lane == part + 1.0], axis=0)
-    found = exact_dot(pick.astype(F32), rows)
-    below = exact_dot(found[8:16], spread[:, :128])
-    above = exact_dot(found[16:24], spread[:, 128:])
+    both = jnp.dot(
+        pick.astype(F32).astype(BF16), jnp.concatenate(split(rows), axis=1),
+        preferred_element_type=F32,
+    )
+    found = both[:, :128] + both[:, 128:]
+    met = two_dot(found[8:], spread)
+    below, above = met[:8, :128], met[8:, 128:]
     count = iota((8, 128), 1)
     base = ((count // 16) == uv).astype(F32)
     own = (count % 2).astype(F32) == parity
@@ -315,31 +320,46 @@
 
 
 def phase_spectrum(c):
-    pattern = (c.phase[...] == 1).astype(F32).astype(BF16)
-    z = jnp.dot(c.lf_h[:, :256], pattern, preferred_element_type=F32)
-    z = z + jnp.dot(c.lf_l[:, :256], pattern, preferred_element_type=F32)
+    pattern = (c.phase[...] == 1).astype(F32)
+    halves = (pattern[:128] + pattern[128:], pattern[:128] - pattern[128:])
+    z = []
+    for odd in range(2):
+        half = halves[odd].astype(BF16)
+        one = jnp.dot(c.lf_h[odd, :, :128], half, preferred_element_type=F32)
+        z.append(one + jnp.dot(c.lf_l[odd, :, :128], half, preferred_element_type=F32))
     for k in range(8):
-        rows = jnp.concatenate([z[32 * k : 32 * k + 32], z[256 + 32 * k : 288 + 32 * k]], axis=1)
+        rows = jnp.concatenate(
+            [
+                jnp.concatenate([v[16 * k : 16 * k + 16], v[128 + 16 * k : 144 + 16 * k]], axis=1)
+                for v in z
+            ],
+            axis=0,
+        )
         high, low = split(rows)
-        c.chi[pl.ds(32 * k, 32), :] = dot3(high, low, c.rf_h[k], c.rf_l[k])
+        c.chi[32 * k : 32 * k + 32, :] = dot3(high, low, c.rf_h[k], c.rf_l[k])
 
 
 def back_right(c, k):
-    high, low = split(c.spec[...])
+    high, low = split(c.spec[k])
     w = dot3(high, low, c.ri_h[k], c.ri_l[k])
     high, low = split(w)
     for q in range(6):
-        for part in range(2):
-            at = (pl.ds(pl.multiple_of(256 * part + 32 * k, 32), 32), pl.ds(128 * q, 128))
-            from_ = (slice(32 * q, 32 * q + 32), slice(128 * part, 128 * part + 128))
-            c.x_h[at] = high[from_]
-            c.x_l[at] = low[from_]
+        for odd in range(2):
+            for part in range(2):
+                at = 256 * odd + 128 * part + 16 * k
+                at = (slice(at, at + 16), slice(128 * q, 128 * q + 128))
+                lead = 32 * q + 16 * odd
+                from_ = (slice(lead, lead + 16), slice(128 * part, 128 * part + 128))
+                c.x_h[at] = high[from_]
+                c.x_l[at] = low[from_]
 
 
 def left(c, high, low, out):
-    for q in range(3):
-        cols = pl.ds(256 * q, 256)
-        out[:, cols] = dot3(high[...], low[...], c.x_h[:, cols], c.x_l[:, cols])
+    for odd in range(2):
+        rows = slice(256 * odd, 256 * odd + 256)
+        for q in range(3):
+            cols = slice(256 * q, 256 * q + 256)
+            out[rows, cols] = dot3(high[odd], low[odd], c.x_h[rows, cols], c.x_l[rows, cols])
 
 
 def solve(c, e, turns):
@@ -351,98 +371,100 @@
             ends.append([stiff * v + (kt if i < 3 else 0.0) for i, v in enumerate(dev)])
         jumps.append([b - a for a, b in zip(*ends)])
 
-    def first(k, carry):
+    for k in range(8):
         for part in range(4):
-            at = pl.multiple_of(32 * k + 8 * part, 8)
-            t = [c.green[q, pl.ds(at, 8), :] for q in range(9)]
-            real, imag = c.chi[pl.ds(at, 8), :128], c.chi[pl.ds(at, 8), 128:]
+            at = 32 * k + 8 * part
+            t = [c.green[q, at : at + 8, :] for q in range(9)]
+            real, imag = c.chi[at : at + 8, :128], c.chi[at : at + 8, 128:]
             one, two = green(jumps[0], t[:6], t[6:]), green(jumps[1], t[:6], t[6:])
             for q in range(6):
                 rows = slice(32 * q + 8 * part, 32 * q + 8 * part + 8)
-                c.spec[rows, :128] = real * one[q] - imag * two[q]
-                c.spec[rows, 128:] = real * two[q] + imag * one[q]
+                c.spec[k, rows, :128] = real * one[q] - imag * two[q]
+                c.spec[k, rows, 128:] = real * two[q] + imag * one[q]
         back_right(c, k)
+    left(c, c.li_h, c.li_l, c.u)
+
+    def halves(ref, lead, r, step):
+        near, far = (pl.ds(pl.multiple_of(at + lead + step * r, step), step) for at in (0, 256))
+        cols = [pl.ds(128 * i, 128) for i in range(6)]
+        even, odd = [ref[near, v] for v in cols], [ref[far, v] for v in cols]
+        return [a + b for a, b in zip(even, odd)], [a - b for a, b in zip(even, odd)]
+
+    def stress(r, carry):
+        for q in range(2):
+            sides = []
+            for side, moved in enumerate(halves(c.u, 128 * q, r, 16)):
+                at = pl.ds(pl.multiple_of(128 * side + 16 * r, 16), 16)
+                kappa, shear, scale = materials(c.phase[at, :] == 1)
+                field = [jnp.concatenate([e[q][i]] * 2, axis=0) - moved[i] for i in range(6)]
+                kt, dev, stiff, _ = law(field, kappa, shear, scale)
+                rows = pl.ds(pl.multiple_of(256 * side + 128 * q + 16 * r, 16), 16)
+                for i in range(6):
+                    c.f[rows, pl.ds(128 * i, 128)] = field[i]
+                sides.append([stiff * dev[i] + (kt if i < 3 else 0.0) for i in range(6)])
+            for i in range(6):
+                for odd in range(2):
+                    a, b = sides[0][i], sides[1][i]
+                    high, low = split(a - b if odd else a + b)
+                    rows = pl.ds(pl.multiple_of(256 * odd + 128 * q + 16 * r, 16), 16)
+                    c.x_h[rows, pl.ds(128 * i, 128)] = high
+                    c.x_l[rows, pl.ds(128 * i, 128)] = low
         return carry
 
-    lax.fori_loop(0, 8, first, 0)
-    left(c, c.li_h, c.li_l, c.u)
-
-    def stress(r, carry):
-        at = pl.multiple_of(16 * r, 16)
-        kappa, shear, scale = materials(c.phase[pl.ds(at, 16), :] == 1)
-        for q in range(2):
-            rows = pl.ds(pl.multiple_of(256 * q + 16 * r, 16), 16)
-            field = [
-                jnp.concatenate([e[q][i]] * 2, axis=0) - c.u[rows, pl.ds(128 * i, 128)]
-                for i in range(6)
-            ]
-            kt, dev, stiff, _ = law(field, kappa, shear, scale)
-            for i in range(6):
-                c.f[rows, pl.ds(128 * i, 128)] = field[i]
-                high, low = split(stiff * dev[i] + (kt if i < 3 else 0.0))
-                c.x_h[rows, pl.ds(128 * i, 128)] = high
-                c.x_l[rows, pl.ds(128 * i, 128)] = low
-        return carry
-
-    lax.fori_loop(0, 16, stress, 0)
+    lax.fori_loop(0, 8, stress, 0)
     left(c, c.lf_h, c.lf_l, c.u)
 
-    def middle(k, carry):
-        near, far = pl.multiple_of(32 * k, 32), pl.multiple_of(256 + 32 * k, 32)
-        rows = jnp.concatenate(
-            [
-                jnp.concatenate(
-                    [c.u[pl.ds(near, 32), pl.ds(128 * q, 128)], c.u[pl.ds(far, 32), pl.ds(128 * q, 128)]],
-                    axis=1,
-                )
-                for q in range(6)
-            ],
-            axis=0,
-        )
-        high, low = split(rows)
-        c.spec[...] = dot3(high, low, c.rf_h[k], c.rf_l[k])
+    for k in range(8):
+        rows = []
+        for q in range(6):
+            cols = slice(128 * q, 128 * q + 128)
+            for odd in range(2):
+                at = 256 * odd + 16 * k
+                pair = [c.u[at : at + 16, cols], c.u[128 + at : 144 + at, cols]]
+                rows.append(jnp.concatenate(pair, axis=1))
+        high, low = split(jnp.concatenate(rows, axis=0))
+        c.spec[k] = dot3(high, low, c.rf_h[k], c.rf_l[k])
         for part in range(4):
-            at = pl.multiple_of(32 * k + 8 * part, 8)
-            t = [c.green[q, pl.ds(at, 8), :] for q in range(9)]
+            at = 32 * k + 8 * part
+            t = [c.green[q, at : at + 8, :] for q in range(9)]
             for half in range(2):
                 cols = slice(128 * half, 128 * half + 128)
                 spots = [slice(32 * q + 8 * part, 32 * q + 8 * part + 8) for q in range(6)]
-                out = green([c.spec[s, cols] for s in spots], t[:6], t[6:])
-                for s, v in zip(spots, out):
-                    c.spec[s, cols] = v
+                out = green([c.spec[k, v, cols] for v in spots], t[:6], t[6:])
+                for v, new in zip(spots, out):
+                    c.spec[k, v, cols] = new
         back_right(c, k)
-        return carry
-
-    lax.fori_loop(0, 8, middle, 0)
     left(c, c.li_h, c.li_l, c.u)
 
     for q in range(2):
         keep = jnp.broadcast_to((turns[q] > 1.5).astype(F32), (8, 128))
 
         def total(r, sums, q=q, keep=keep):
-            at = pl.multiple_of(8 * r, 8)
-            kappa, shear, scale = materials(c.phase[pl.ds(at, 8), :] == 1)
-            rows = pl.ds(pl.multiple_of(256 * q + 8 * r, 8), 8)
-            field = [
-                c.f[rows, pl.ds(128 * i, 128)] - keep * c.u[rows, pl.ds(128 * i, 128)]
-                for i in range(6)
-            ]
-            kt, dev, stiff, factor = law(field, kappa, shear, scale)
-            weight = stiff * factor * factor * scale
-            heavy = [weight * v for v in dev]
-            new = [kt] + [stiff * v for v in dev] + [shear * factor]
-            new += [heavy[i] * dev[j] for i, j in UPPER] + [kappa]
-            return tuple(s + v for s, v in zip(sums, new))
-
-        sums = lax.fori_loop(0, 32, total, (jnp.zeros((8, 128), F32),) * 30)
+            for side, moved in enumerate(halves(c.u, 128 * q, r, 8)):
+                at = pl.ds(pl.multiple_of(128 * side + 8 * r, 8), 8)
+                kappa, shear, scale = materials(c.phase[at, :] == 1)
+                rows = pl.ds(pl.multiple_of(256 * side + 128 * q + 8 * r, 8), 8)
+                field = [c.f[rows, pl.ds(128 * i, 128)] - keep * moved[i] for i in range(6)]
+                kt, dev, stiff, factor = law(field, kappa, shear, scale)
+                weight = stiff * factor * factor * scale
+                heavy = [weight * v for v in dev]
+                new = [kt] + [stiff * v for v in dev] + [shear * factor]
+                new += [heavy[i] * dev[j] for i, j in UPPER] + [kappa]
+                sums = tuple(s + v for s, v in zip(sums, new))
+            return sums
+
+        sums = lax.fori_loop(0, 16, total, (jnp.zeros((8, 128), F32),) * 30)
         for n, v in enumerate(sums):
-            c.sums[pl.ds(256 * q + 8 * n, 8), :] = v
-        c.sums[pl.ds(256 * q + 240, 16), :] = jnp.zeros((16, 128), F32)
-    ones = jnp.ones((8, 128), F32)
-    lanes = lax.dot_general(
-        ones, c.sums[...], (((1,), (1,)), ((), ())), precision=EXACT, preferred_element_type=F32
-    )
-    return exact_dot(lanes, c.summary[...])
+            c.sums[256 * q + 8 * n : 256 * q + 8 * n + 8, :] = v
+        c.sums[256 * q + 240 : 256 * q + 256, :] = jnp.zeros((16, 128), F32)
+    ones = jnp.ones((8, 128), BF16)
+    across = (((1,), (1,)), ((), ()))
+    lanes = [
+        lax.dot_general(ones, v, across, preferred_element_type=F32) for v in split(c.sums[...])
+    ]
+    high, low = split(lanes[0] + lanes[1])
+    out = jnp.dot(jnp.concatenate([high, low]), c.summary[0], preferred_element_type=F32)
+    return out[:8] + out[8:] + jnp.dot(high, c.summary[1], preferred_element_type=F32)
 
 
 def finish(c, listed, out_ref):
@@ -452,7 +474,22 @@
     point = (2 * (jnp.full((8, 128), dev, jnp.int32) + step) + sub % 2).astype(F32)
     point = jnp.where(sub < 6, point, NONE)
     found, masked = point_rows(c.rows[...], point, 1, c.small[:, 1024:1280])
-    direction = exact_dot(masked, c.small[:, 1280:1408])
+    factor = jnp.where(lane < 6, 1.0, two_dot(masked, c.small[:, 1280:1408]))
+    linked = [
+        jnp.where((lane // 16 == sub + lead) & (sub < 3), found[at : at + 1], 0.0)
+        for at, lead in ((2, 5), (4, 2))
+    ]
+    parts = jnp.concatenate([c.near[n] for n in range(4)] + linked, axis=0)
+    spread = two_dot(parts, c.small[:, 1408:1664])
+    weights = []
+    for n in range(6):
+        first = 2 * max(0, n - 3)
+        weights.append(
+            [
+                spread[8 * n : 8 * n + 8, 128 * p : 128 * p + 128] * factor[first + p : first + p + 1]
+                for p in range(2)
+            ]
+        )
     index = iota((8, 256), 1).astype(F32)
     wide = jnp.concatenate([point, point], axis=1)
     owners = jnp.broadcast_to(c.owner[...].astype(F32), (8, 256))
@@ -462,11 +499,15 @@
     )
     slot = jnp.floor(rank * 0.5)
     core = jnp.full((8, 1), grp, jnp.int32).astype(F32)
-    ours = (rank - 2.0 * slot) == core
-    pick = ((lanes_f32() == who) & ours).astype(F32)
+    place = jnp.where((rank - 2.0 * slot) == core, who, NONE)
+    row = iota((128, 128), 0).astype(F32)
 
     gather_wait(c.results, c.send_b, c.recv_b)
-    value = exact_dot(pick, c.results[...])
+    results = c.results[...]
+    value = jnp.zeros((8, 128), F32)
+    for q in range(6):
+        one = jnp.sum(jnp.where(row == place[q : q + 1], results, 0.0), axis=0, keepdims=True)
+        value = jnp.where(sub == q, one, value)
     value = jnp.where(slot > 0.5, pltpu.roll(value, 64, 1), value)
     value = jnp.where(lane < 64, value, 0.0)
     c.swap[0] = value
@@ -478,40 +519,36 @@
     copy.wait()
     value = value + c.swap[1]
     out_ref[0] = value
-    terms = value * jnp.where(lane < 6, 1.0, direction)
-    dealt = exact_dot(terms, c.small[:, 1408:1664])
-    own_lane = lane % 2 == sub % 2
-    twelve = lane % 16 < 12
+    sums = []
+    for n in range(6):
+        first = 2 * max(0, n - 3)
+        a, b = weights[n]
+        sums.append(a * value[first : first + 1] + b * value[first + 1 : first + 2])
     for half in range(2):
-        y = jnp.where(own_lane, dealt[:, 128 * half : 128 * half + 128], 0.0)
-        mine = jnp.sum(jnp.where(sub < 2, y, 0.0), axis=0, keepdims=True)
-        linked = y * found
-        before = jnp.sum(jnp.where((sub == 2) | (sub == 3), linked, 0.0), axis=0, keepdims=True)
-        after = jnp.sum(jnp.where((sub == 4) | (sub == 5), linked, 0.0), axis=0, keepdims=True)
         out = jnp.zeros((8, 128), F32)
-        for n in range(4):
-            got = jnp.sum(c.near[n] * jnp.where(lane < 12, mine, 0.0), axis=1, keepdims=True)
-            out = jnp.where(lane == n, got, out)
-        for end, row, lead in ((0, before, 5), (1, after, 2)):
-            part = jnp.where(twelve & (lane // 16 == sub + lead) & (sub < 3), row, 0.0)
-            got = jnp.sum(part, axis=1, keepdims=True)
-            out = out + jnp.where(lane == listed[end], got, 0.0)
+        mine = (lane >= 8) if half else (lane < 8)
+        for n in range(6):
+            got = jnp.sum(jnp.where(mine, sums[n], 0.0), axis=1, keepdims=True)
+            if n < 4:
+                out = jnp.where(lane == n, got, out)
+            else:
+                out = out + jnp.where(lane == listed[n - 4], got, 0.0)
         out_ref[1 + half] = out
 
 
 TABLES = {
-    "lf": ((2, 512, 512), BF16),
+    "lf": ((2, 2, 256, 256), BF16),
     "rf": ((2, 8, 256, 256), BF16),
-    "li": ((2, 512, 512), BF16),
+    "li": ((2, 2, 256, 256), BF16),
     "ri": ((2, 8, 256, 256), BF16),
     "green": ((9, 256, 128), F32),
-    "small": ((128, 1664), F32),
-    "summary": ((512, 128), F32),
+    "small": ((128, 1664), BF16),
+    "summary": ((2, 512, 128), BF16),
     "phase": ((256, 128), jnp.int32),
 }
 WORK = {
     "chi": ((256, 256), F32),
-    "spec": ((192, 256), F32),
+    "spec": ((8, 192, 256), F32),
     "x_h": ((512, 768), BF16),
     "x_l": ((512, 768), BF16),
     "u": ((512, 768), F32),
@@ -535,15 +572,15 @@
 
 def constants():
     out = dict(zip(("lf", "rf", "li", "ri"), (np.stack(two_parts(t)) for t in dft_tables())))
-    spread_u, splat, spread_v, expand, deal = message_tables()
-    out["small"] = np.concatenate([spread_u, splat, spread_v, expand, deal], axis=1)
-    out["green"], out["summary"] = green_tables(), summary_table()
+    small = np.concatenate(message_tables(), axis=1)
+    out["small"] = small.astype(ml_dtypes.bfloat16)
+    out["green"], out["summary"] = green_tables(), np.stack(two_parts(summary_table()))
     return out
 
 
 def splats(c, point):
     _, masked = point_rows(c.rows[...], point, 0, c.small[:, :256])
-    strain = exact_dot(masked, c.small[:, 256:1024])
+    strain = two_dot(masked, c.small[:, 256:1024])
     return [
         [jnp.broadcast_to(strain[q : q + 1, 128 * i : 128 * i + 128], (8, 128)) for i in range(6)]
         for q in range(2)
@@ -601,7 +638,7 @@
         + [pltpu.SemaphoreType.DMA] * len(SEMS)
         + [pltpu.SemaphoreType.DMA((8,))],
         compiler_params=pltpu.CompilerParams(
-            collective_id=0, has_side_effects=True, vmem_limit_bytes=48 << 20
+            collective_id=0, has_side_effects=True, vmem_limit_bytes=63 << 20
         ),
     )(
         disp, probe, strain_disp.transpose(0, 2, 1), conn.T, halo_rows,

time: 63.6 us -> 42.1 us (0.66)
  local copies, waits for them, and re-layouts: 12.1 us -> 0 us
  Pallas kernels: 50.4 us -> 41.3 us
    unnamed x28 -> x0, local copies, waits for them, and re-layouts: 12.1 us -> none
    pallas_call x1, Pallas kernels: 49.1 us -> 40 us  [on_device(): pl.pallas_call(main_kernel, out_shape=shape((3, 8, 128), F32), in_specs=[...]
where the time goes in v3:
time: 42.1 us; the launch traced here: 42 us
  Pallas kernels  41.3 us (98%)
  between operations  0.64 us (2%)
    pallas_call x1, Pallas kernels, on_device(): pl.pallas_call(main_kernel, out_shape=shape((3, 8, 128), F32), in_specs=[...  40 us
    pallas_call x1, Pallas kernels, on_device(): pl.pallas_call(last_kernel, out_shape=(shape((2, 6), F32), shape((3, 4),...  1.3 us

profile of v3, /device:TPU:1, one launch (start us, length us, event | category | flops | bytes accessed | tf_op | source)
XLA Modules:
  0.0 42.0 jit_solution(15759588743251521522)
XLA Ops:
  0.6 40.0 %shard_map.166.packed = f32[3,8,128]{2,1,0:T(8,128)} custom-call(f32[3,4]{1,0:T(4,128)} %refs_0_.1, f32[3,4]{1,0:T(4,128)} %refs_1_.1, f32[6,2,24]{2,1,0:T(2,128)} %bitcast.7, s32[2,8]{1,0:T(2,128)} %bitcast.8, s32[2]{0:T(128)} %refs_4_.1, s32[1,256]{1,0:T(1,128)} %bitcast.9, s32[1,256]{1,0:T(1,128)} %bitcast.10, ...), custom_call_target="tpu_custom_call" | custom-call | tf_op jit(solution)/shard_map/pallas_call | solution.py:631
  40.7 1.3 %shard_map.167 = (f32[2,6]{1,0:T(2,128)}, f32[3,4]{1,0:T(4,128)}, f32[3,4]{1,0:T(4,128)}) custom-call(f32[3,8,128]{2,1,0:T(8,128)} %shard_map.166.packed), custom_call_target="tpu_custom_call" | custom-call | tf_op jit(solution)/shard_map/pallas_call | solution.py:647
